TPU v7x, 256 devices: a whole 4x4x8 slice. The times are simulated.
256 devices in a mesh: lat: 16 (over z, core), lon: 16 (over x, y).
Axes of the slice: x: 4, y: 4, z: 8, core: 2. Of those that a mesh axis runs over, the one named last changes fastest.
Arguments:
- ensemble: float32 [3, 80, 512, 2048], P(None, None, 'lat', 'lon'), may hold values from -6 to 6
- courant_cols: float32 [1, 512, 2048], P(None, 'lat', 'lon'), may hold values from -0.6 to 0.6
- courant_rows: float32 [1, 512, 2048], P(None, 'lat', 'lon'), may hold values from -0.6 to 0.6
- obs_value: float32 [2, 6144], P(None, ('lat', 'lon')), may hold values from -8 to 8
- obs_error: float32 [2, 6144], P(None, ('lat', 'lon')), may hold values from 0.2 to 2
- obs_cell: int32 [2, 6144], P(None, ('lat', 'lon')), may hold values from 0 to 4095
- obs_kind: int32 [2, 6144], P(None, ('lat', 'lon')), may hold values from 0 to 2
- obs_live: int32 [2, 6144], P(None, ('lat', 'lon')), may hold values from 0 to 1, as said below
- obs_list: int32 [2, 6144, 9], P(None, ('lat', 'lon')), may hold values 0 or 1
Outputs:
- analysis: float32 [3, 80, 512, 2048], P(None, None, 'lat', 'lon')
Inputs may be any that keep to these rules, and one draw needn't show every extreme that they name: `obs_live`: in each batch the live slots of a tile are its first ones, and in every batch some tile has all 24 slots live.
All inputs are finite; a program needn't handle non-finite values. No bound on the sum of `obs_list` on one device may be relied on, other than what follows from the above.
Results may differ from a plain program's by a relative error of at most 0.0003.
Values sent between devices are 32-bit elements; how exact they have to be, the bound alone decides.
No kernel may reach another device: no remote copies, remote signals or barrier semaphores. Data moves between devices by JAX's collectives and lax.ppermute only.
A program may use at most 64 MiB of HBM per device.

v0:
```python
import jax
import jax.numpy as jnp
from jax import lax
from jax.experimental import pallas as pl
from jax.experimental.pallas import tpu as pltpu
from jax.sharding import PartitionSpec as P

F, M, R, C, K = 3, 80, 32, 128, 24
GAIN, INNOV, ALPHA, ROW, COL, LIST = 80, 81, 82, 83, 84, 96
S = 80
f32, bf16 = jnp.float32, jnp.bfloat16
VMEM = pltpu.VMEM
MiB = 1 << 20


def lanes(shape):
    return lax.broadcasted_iota(jnp.int32, shape, len(shape) - 1)


def split(x):
    hi = x.astype(bf16)
    return hi, (x - hi.astype(f32)).astype(bf16)


def split3(x):
    hi = x.astype(bf16)
    rest = x - hi.astype(f32)
    mid = rest.astype(bf16)
    return hi, mid, (rest - mid.astype(f32)).astype(bf16)


def dot(a, b, dims=((1,), (0,))):
    return lax.dot_general(a, b, (dims, ((), ())), preferred_element_type=f32)


def edges_kernel(par, x_hbm, xt, row_a, row_b, col_a, col_b, buf, acc, sem):
    for ib in range(R // 8):
        for f in range(F):
            pltpu.make_async_copy(
                x_hbm.at[f, :, pl.ds(ib * 8, 8), :], buf.at[ib, f], sem.at[ib, f]
            ).start()
    acc[...] = jnp.zeros_like(acc)
    lane = lanes((M, C))
    for ib in range(R // 8):
        for f in range(F):
            pltpu.make_async_copy(
                x_hbm.at[f, :, pl.ds(ib * 8, 8), :], buf.at[ib, f], sem.at[ib, f]
            ).wait()
            rows = buf.at[ib, f].reshape(M * 8, C)
            first, last = acc[0], acc[1]
            for r in range(8):
                v = rows[pl.ds(r, M, stride=8), :]
                i = ib * 8 + r
                k = f * R + i
                xt[f, i] = v
                turned = pltpu.roll(v, k, 1) if k else v
                first = jnp.where(lane == k, turned, first)
                last = jnp.where(lane == (k - 1) % C, turned, last)
            acc[0] = first
            acc[1] = last
    first, last = acc[0], pltpu.roll(acc[1], 1, 1)
    odd = (jnp.zeros((M, C), jnp.int32) + par[1]) == 1
    col_a[...] = jnp.where(odd, first, last)
    col_b[...] = jnp.where(odd, last, first)
    ra = jnp.where(par[0] == 1, 0, R - 1)
    rb = R - 1 - ra
    for f in range(F):
        row_a[f] = xt[f, ra]
        row_b[f] = xt[f, rb]


def observe(b, state, cell, kind, value, error, live, listed, table):
    lane = lanes((M, C))
    prior = jnp.zeros((M, C), f32)
    lane1 = lanes((1, C))
    row = jnp.zeros((1, C), f32)
    col = jnp.zeros((1, C), f32)
    for s in range(K):
        at = cell[b, s]
        r, c = at // C, at % C
        v = state[kind[b, s], r]
        prior = jnp.where(lane == s, pltpu.roll(v, (s + C - c) % C, 1), prior)
        row = jnp.where(lane1 == s, r.astype(f32), row)
        col = jnp.where(lane1 == s, c.astype(f32), col)
    ybar = jnp.sum(prior, axis=0, keepdims=True) / M
    yp = prior - ybar
    spread = jnp.sum(yp * yp, axis=0, keepdims=True) / (M - 1)
    err = error[b : b + 1, :]
    total = spread + err
    gain = live[b : b + 1, :] / total
    alpha = 1.0 / (1.0 + jnp.sqrt(err / total))
    innov = value[b : b + 1, :] - ybar
    sub = lax.broadcasted_iota(jnp.int32, (16, C), 0)
    extra = jnp.zeros((16, C), f32)
    for n, v in enumerate((gain, innov, alpha, row, col)):
        extra = jnp.where(sub == n, v, extra)
    whole = jnp.concatenate([yp, extra, jnp.zeros((32, C), f32)], axis=0)
    table[...] = whole.T[:K] + listed[b]


def advect_kernel(
    par, cell, kind, xt, row_a, row_b, col_a, col_b, cc, cr, value, error, live, listed,
    state, table, merged,
):
    lane = lanes((M, C))
    odd_lane = (lane % 2) == 1
    odd_b = (jnp.zeros((M, C), jnp.int32) + par[1]) == 1
    got_a, got_b = col_a[...], col_b[...]
    east = pltpu.roll(jnp.where(odd_b, got_b, got_a), C - 1, 1)
    west = jnp.where(odd_b, got_a, got_b)
    merged[0] = jnp.where(odd_lane, east, west)
    merged[1] = jnp.where(odd_lane, west, east)
    odd_a = (jnp.zeros((M, C), jnp.int32) + par[0]) == 1

    def one(i, parity, low, high):
        u = cc[0, pl.ds(i, 1), :]
        v = cr[0, pl.ds(i, 1), :]
        uu, vv = 0.5 * u * u, 0.5 * v * v
        here = 1.0 - 2.0 * uu - 2.0 * vv
        ae, aw = uu - 0.5 * u, uu + 0.5 * u
        an, as_ = vv - 0.5 * v, vv + 0.5 * v
        for f in range(F):
            x = xt[f, i]
            k = f * R + i
            halo = pltpu.roll(merged[parity], (C - k) % C, 1)
            xe = jnp.where(lane == C - 1, halo, pltpu.roll(x, C - 1, 1))
            xw = jnp.where(lane == 0, halo, pltpu.roll(x, 1, 1))
            if low:
                xs = jnp.where(odd_a, row_a[f], row_b[f])
            else:
                xs = xt[f, i - 1]
            if high:
                xn = jnp.where(odd_a, row_b[f], row_a[f])
            else:
                xn = xt[f, i + 1]
            state[f, i] = here * x + ae * xe + aw * xw + an * xn + as_ * xs

    one(0, 0, True, False)
    one(R - 1, 1, False, True)

    def body(n, carry):
        one(2 * n + 1, 1, False, False)
        one(2 * n + 2, 0, False, False)
        return carry

    lax.fori_loop(0, R // 2 - 1, body, 0)
    observe(0, state, cell, kind, value, error, live, listed, table)


def gather_tables(par, own, side_a, side_b, full):
    sa = 1 - 2 * par[0]
    sb = 1 - 2 * par[1]
    lane = lanes((K, C))
    actives = []
    for q, src in enumerate((own, side_a, side_b)):
        db = (0, sb, -sb)[q]
        for p in range(3):
            da = (0, sa, -sa)[p]
            t = src[pl.ds(p * K, K), :]
            slot = LIST + (1 - da) * 3 + (1 - db)
            chosen = jnp.sum(jnp.where(lane == slot, t, 0.0), axis=1, keepdims=True)
            factor = t[:, GAIN : GAIN + 1] * chosen
            row = t[:, ROW : ROW + 1] + jnp.asarray(da * R, f32)
            col = t[:, COL : COL + 1] + jnp.asarray(db * C, f32)
            t = jnp.where(lane == GAIN, factor, t)
            t = jnp.where(lane == ROW, row, t)
            t = jnp.where(lane == COL, col, t)
            n = (q * 3 + p) * K
            full[n : n + K, :] = t
            near = (row > -float(R)) & (row < 2.0 * R - 1.0) & (col > -float(R)) & (col < C + R - 1.0)
            actives.append(jnp.where(near & (factor != 0.0), 1.0, 0.0))
    return jnp.concatenate(actives, axis=0)


def spread_lanes(hi, lo):
    r = lax.broadcasted_iota(jnp.int32, (C, 2 * C), 0)
    c = lax.broadcasted_iota(jnp.int32, (C, 2 * C), 1)
    keep = r < S
    e_hi = (((c == r) | (c == r + 2 * S)) & keep).astype(f32).astype(bf16)
    e_lo = ((c == r + S) & keep).astype(f32).astype(bf16)
    return (dot(hi, e_hi) + dot(lo, e_lo)).astype(bf16)


def compact(active, full, chunk, ycat, bcat, col_w, row_b, fac_b):
    n = 9 * K
    act = jnp.broadcast_to(active, (n, C))
    tri = (
        lax.broadcasted_iota(jnp.int32, (n, n), 1) < lax.broadcasted_iota(jnp.int32, (n, n), 0)
    ).astype(f32).astype(bf16)
    rank = dot(tri, act.astype(bf16)).astype(jnp.int32) - chunk * S
    lane = lanes((n, C))
    pick = ((rank == lane) & (act > 0.0) & (lane < S)).astype(f32).astype(bf16)
    parts = split3(full[...])
    over = ((0,), (0,))
    chosen = sum(dot(pick, t, over) for t in parts)[:S]
    turned = sum(dot(t, pick, over) for t in parts)
    ycat[...] = spread_lanes(*split(chosen))
    back = turned[INNOV : INNOV + 1, :] - turned[ALPHA : ALPHA + 1, :] * turned[:M]
    bcat[...] = spread_lanes(*split(back))
    col = jnp.broadcast_to(chosen[:, COL : COL + 1], (S, C))
    row_b[...] = jnp.broadcast_to(chosen[:, ROW : ROW + 1], (S, C))
    fac_b[...] = jnp.broadcast_to(chosen[:, GAIN : GAIN + 1], (S, C)) / (M - 1)
    z = jnp.maximum(0.0, 1.0 - jnp.abs(col - lanes((S, C)).astype(f32)) / R)
    col_w[...] = z * z


def localize(i, col_w, row_b, fac_b):
    z = jnp.maximum(0.0, 1.0 - jnp.abs(row_b[...] - i.astype(f32)) / R)
    return z * z * fac_b[...] * col_w[...]


def update(p, lw, ycat, bcat):
    hi, lo = split(p)
    proj = dot(ycat[...], jnp.concatenate([hi, hi, lo, jnp.zeros((16, 2 * C), bf16)], axis=0))
    hi, lo = split(proj * lw)
    return dot(bcat[...], jnp.concatenate([hi, hi, lo, jnp.zeros((16, 2 * C), bf16)], axis=0))


def assimilate(par, own, side_a, side_b, state, scratch, emit, gather_base):
    full, ycat, bcat, col_w, row_b, fac_b, total = scratch
    active = gather_tables(par, own, side_a, side_b, full)
    count = jnp.sum(active).astype(jnp.int32)

    def sweep(base, put):
        def body(n, carry):
            i = 2 * n
            lw = jnp.concatenate(
                [localize(i, col_w, row_b, fac_b), localize(i + 1, col_w, row_b, fac_b)], axis=1
            )
            for f in range(F):
                p = jnp.concatenate([state[f, i], state[f, i + 1]], axis=1)
                d = update(p, lw, ycat, bcat)
                put(n, f, base[f, i] + d[:, :C], base[f, i + 1] + d[:, C:])
            return carry

        return body

    def keep(n, f, a, b):
        total[f, 2 * n] = a
        total[f, 2 * n + 1] = b

    compact_args = (ycat, bcat, col_w, row_b, fac_b)

    @pl.when(count > S)
    def _():
        def chunk(j, carry):
            compact(active, full, j, *compact_args)

            @pl.when(j == 1)
            def _():
                lax.fori_loop(0, R // 2, sweep(state, keep), 0)

            @pl.when(j > 1)
            def _():
                lax.fori_loop(0, R // 2, sweep(total, keep), 0)

            return carry

        lax.fori_loop(1, (count + S - 1) // S, chunk, 0)
        compact(active, full, 0, *compact_args)
        emit(sweep, total)

    @pl.when(count <= S)
    def _():
        compact(active, full, 0, *compact_args)
        emit(sweep, state)


def first_kernel(
    par, cell, kind, own, side_a, side_b, state, value, error, live, listed, out, table, *scratch
):
    def emit(sweep, base):
        def put(n, f, a, b):
            out[f, 2 * n] = a
            out[f, 2 * n + 1] = b

        lax.fori_loop(0, R // 2, sweep(base, put), 0)

    assimilate(par, own, side_a, side_b, state, scratch, emit, None)
    observe(1, out, cell, kind, value, error, live, listed, table)


def second_kernel(par, own, side_a, side_b, state, out, *rest):
    buf, sem, scratch = rest[0], rest[1], rest[2:]

    def copy(ib, f):
        return pltpu.make_async_copy(
            buf.at[ib, f], out.at[f, :, pl.ds(ib * 8, 8), :], sem.at[ib, f]
        )

    def emit(sweep, base):
        for ib in range(R // 8):

            def put(n, f, a, b):
                rows = buf.at[ib, f].reshape(M * 8, C)
                r = 2 * (n - 4 * ib)
                rows[pl.ds(r, M, stride=8), :] = a
                rows[pl.ds(r + 1, M, stride=8), :] = b

            lax.fori_loop(4 * ib, 4 * ib + 4, sweep(base, put), 0)
            for f in range(F):
                copy(ib, f).start()

    assimilate(par, own, side_a, side_b, state, scratch, emit, None)
    for ib in range(R // 8):
        for f in range(F):
            copy(ib, f).wait()


def spec(space):
    return pl.BlockSpec(memory_space=space)


def call(kernel, outs, args, spaces, out_spaces, scratch, name):
    return pl.pallas_call(
        kernel,
        out_shape=outs,
        in_specs=[spec(s) for s in spaces],
        out_specs=[spec(s) for s in out_spaces],
        scratch_shapes=scratch,
        compiler_params=pltpu.CompilerParams(vmem_limit_bytes=40 * MiB),
        name=name,
    )(*args)


def swap(x, axis, shift):
    n = lax.axis_size(axis)
    pairs = [(i, ((i - shift) ^ 1) + shift) for i in range(n)]
    pairs = [(i, j) for i, j in pairs if i >= shift and 0 <= j < n]
    return lax.ppermute(x, axis, pairs)


def on_device(
    ensemble, courant_cols, courant_rows, obs_value, obs_error, obs_cell, obs_kind, obs_live, obs_list
):
    par = jnp.stack([lax.axis_index("lat") % 2, lax.axis_index("lon") % 2]).astype(jnp.int32)
    pad = ((0, 0), (0, C - K))
    value = jnp.pad(obs_value, pad)
    error = jnp.pad(obs_error, pad, constant_values=1.0)
    live = jnp.pad(obs_live.astype(f32), pad)
    listed = jnp.pad(obs_list.astype(f32), ((0, 0), (0, 0), (LIST, C - LIST - 9)))
    SM, HBM = pltpu.SMEM, pltpu.HBM
    block = VMEM((F, R, M, C), f32)
    sds = jax.ShapeDtypeStruct
    table_shape = sds((K, C), f32)

    xt, row_a, row_b, col_a, col_b = call(
        edges_kernel,
        [block, sds((F, M, C), f32), sds((F, M, C), f32), sds((M, C), f32), sds((M, C), f32)],
        [par, ensemble],
        [SM, HBM],
        [VMEM] * 5,
        [VMEM((R // 8, F, M, 8, C), f32), VMEM((2, M, C), f32), pltpu.SemaphoreType.DMA((R // 8, F))],
        "edges",
    )
    row_a, row_b = swap(row_a, "lat", 0), swap(row_b, "lat", 1)
    col_a, col_b = swap(col_a, "lon", 0), swap(col_b, "lon", 1)
    state, table = call(
        advect_kernel,
        [block, table_shape],
        [par, obs_cell, obs_kind, xt, row_a, row_b, col_a, col_b, courant_cols, courant_rows,
         value, error, live, listed],
        [SM] * 3 + [VMEM] * 11,
        [VMEM] * 2,
        [VMEM((2, M, C), f32)],
        "advect",
    )

    def exchange(table):
        own = jnp.concatenate([table, swap(table, "lat", 0), swap(table, "lat", 1)], axis=0)
        return own, swap(own, "lon", 0), swap(own, "lon", 1)

    scratch = [
        VMEM((9 * K, C), f32),
        VMEM((S, 2 * C), bf16),
        VMEM((M, 2 * C), bf16),
        VMEM((S, C), f32),
        VMEM((S, C), f32),
        VMEM((S, C), f32),
        VMEM((F, R, M, C), f32),
    ]
    state, table = call(
        first_kernel,
        [block, table_shape],
        [par, obs_cell, obs_kind, *exchange(table), state, value, error, live, listed],
        [SM] * 3 + [VMEM] * 8,
        [VMEM] * 2,
        scratch,
        "first",
    )
    return call(
        second_kernel,
        [sds((F, M, R, C), f32)],
        [par, *exchange(table), state],
        [SM] + [VMEM] * 4,
        [HBM],
        [VMEM((R // 8, F, M, 8, C), f32), pltpu.SemaphoreType.DMA((R // 8, F))] + scratch,
        "second",
    )[0]


def solution(mesh):
    tiles = P(None, ("lat", "lon"))
    placed = (
        P(None, None, "lat", "lon"),
        P(None, "lat", "lon"),
        P(None, "lat", "lon"),
        tiles,
        tiles,
        tiles,
        tiles,
        tiles,
        P(None, ("lat", "lon"), None),
    )
    return jax.shard_map(
        on_device,
        mesh=mesh,
        in_specs=placed,
        out_specs=P(None, None, "lat", "lon"),
        check_vma=False,
    )
```

profile of v0, /device:TPU:134, one launch (start us, length us, event | category | flops | bytes accessed | tf_op | source)
XLA Modules:
  0.0 74.0 jit_solution(8069776391957038914)
XLA Ops:
  0.1 0.1 pad_add_fusion.par
  0.2 2.1 %copy-done = f32[3,80,32,128]{3,2,1,0:T(8,128)S(1)} copy-done((f32[3,80,32,128]{3,2,1,0:T(8,128)S(1)}, f32[3,80,32,128]{3,2,1,0:T(8,128)}, u32[]{:S(2)}) %copy-start) | copy-done | bytes 3932184
  2.3 3.1 %edges.1 = (f32[3,32,80,128]{3,2,1,0:T(8,128)S(1)}, f32[3,80,128]{2,1,0:T(8,128)S(1)}, f32[3,80,128]{2,1,0:T(8,128)S(1)}, f32[80,128]{1,0:T(8,128)S(1)}, f32[80,128]{1,0:T(8,128)S(1)}) custom-call(s32[2]{0:T(128)S(1)} %pad_add_fusion.par, f32[3,80,32,128]{3,2,1,0:T(8,128)S(1)} %copy-done), custom_call_target="tpu_custom_call" | custom-call | tf_op jit(solution)/shard_map/edges/pallas_call | solution.py:315
  5.4 0.0 copy-start.1
  5.4 1.9 %copy-done.1 = f32[3,32,80,128]{3,2,1,0:T(8,128)} copy-done((f32[3,32,80,128]{3,2,1,0:T(8,128)}, f32[3,32,80,128]{3,2,1,0:T(8,128)S(1)}, u32[]{:S(2)}) %copy-start.1) | copy-done | bytes 3932184
  7.3 2.1 %collective-permute-start.1 = (f32[3,80,128]{2,1,0:T(8,128)S(1)}, f32[3,80,128]{2,1,0:T(8,128)S(1)}, u32[]{:S(2)}, u32[]{:S(2)}) collective-permute-start(f32[3,80,128]{2,1,0:T(8,128)S(1)} %get-tuple-element.16), channel_id=1, source_target_pairs={{16,32},{32,16},{48,64},{64,48},{80,96},{96,80},{112,128},{128,112... | collective-permute-start | bytes 368648 | tf_op jit(solution)/shard_map/ppermute | solution.py:330
  9.4 1.7 %collective-permute-start.2 = (f32[80,128]{1,0:T(8,128)S(1)}, f32[80,128]{1,0:T(8,128)S(1)}, u32[]{:S(2)}, u32[]{:S(2)}) collective-permute-start(f32[80,128]{1,0:T(8,128)S(1)} %get-tuple-element.17), channel_id=1, source_target_pairs={{0,1},{1,0},{2,3},{3,2},{4,5},{5,4},{6,7},{7,6},{8,9},{9,8},{10,11... | collective-permute-start | bytes 122888 | tf_op jit(solution)/shard_map/ppermute | solution.py:330
  11.1 4.3 %collective-permute-start.3 = (f32[80,128]{1,0:T(8,128)S(1)}, f32[80,128]{1,0:T(8,128)S(1)}, u32[]{:S(2)}, u32[]{:S(2)}) collective-permute-start(f32[80,128]{1,0:T(8,128)S(1)} %get-tuple-element.18), channel_id=1, source_target_pairs={{1,2},{2,1},{3,4},{4,3},{5,6},{6,5},{7,8},{8,7},{9,10},{10,9},{11,... | collective-permute-start | bytes 122888 | tf_op jit(solution)/shard_map/ppermute | solution.py:330
  15.5 0.1 copy.10
  15.6 0.1 pad.18.listed
  15.7 3.5 %collective-permute-done.3.col_b = f32[80,128]{1,0:T(8,128)S(1)} collective-permute-done((f32[80,128]{1,0:T(8,128)S(1)}, f32[80,128]{1,0:T(8,128)S(1)}, u32[]{:S(2)}, u32[]{:S(2)}) %collective-permute-start.3) | collective-permute-done | bytes 40992 | tf_op jit(solution)/shard_map/ppermute | solution.py:330
  19.2 0.0 collective-permute-done.1.row_b
  19.2 0.0 copy-start.2
  19.2 2.1 %copy-done.2 = f32[3,32,80,128]{3,2,1,0:T(8,128)S(1)} copy-done((f32[3,32,80,128]{3,2,1,0:T(8,128)S(1)}, f32[3,32,80,128]{3,2,1,0:T(8,128)}, u32[]{:S(2)}) %copy-start.2) | copy-done | bytes 3932184
  21.4 5.4 %advect.1 = (f32[3,32,80,128]{3,2,1,0:T(8,128)S(1)}, f32[24,128]{1,0:T(8,128)S(1)}) custom-call(s32[2]{0:T(128)S(1)} %pad_add_fusion.par, s32[2,24]{1,0:T(2,128)S(1)} %copy-done.5, s32[2,24]{1,0:T(2,128)S(1)} %copy-done.6, f32[3,32,80,128]{3,2,1,0:T(8,128)S(1)} %copy-done.2, f32[3,80,128]{2,1,0:T(8,128)S(1)} %collective-permute-done.row_a, ...), custom_call_target="tpu_custom_call" | custom-call | tf_op jit(solution)/shard_map/advect/pallas_call | solution.py:315
  26.8 3.1 %collective-permute-start.5 = (f32[24,128]{1,0:T(8,128)S(1)}, f32[24,128]{1,0:T(8,128)S(1)}, u32[]{:S(2)}, u32[]{:S(2)}) collective-permute-start(f32[24,128]{1,0:T(8,128)S(1)} %get-tuple-element.19), channel_id=1, source_target_pairs={{16,32},{32,16},{48,64},{64,48},{80,96},{96,80},{112,128},{128,112... | collective-permute-start | bytes 36872 | tf_op jit(solution)/shard_map/ppermute | solution.py:330
  29.9 0.8 %collective-permute-start.4 = (f32[24,128]{1,0:T(8,128)S(1)}, f32[24,128]{1,0:T(8,128)S(1)}, u32[]{:S(2)}, u32[]{:S(2)}) collective-permute-start(f32[24,128]{1,0:T(8,128)S(1)} %get-tuple-element.19), channel_id=1, source_target_pairs={{0,16},{16,0},{32,48},{48,32},{64,80},{80,64},{96,112},{112,96},{1... | collective-permute-start | bytes 36872 | tf_op jit(solution)/shard_map/ppermute | solution.py:330
  30.7 0.8 %collective-permute-done.4 = f32[24,128]{1,0:T(8,128)S(1)} collective-permute-done((f32[24,128]{1,0:T(8,128)S(1)}, f32[24,128]{1,0:T(8,128)S(1)}, u32[]{:S(2)}, u32[]{:S(2)}) %collective-permute-start.4) | collective-permute-done | bytes 12320 | tf_op jit(solution)/shard_map/ppermute | solution.py:330
  31.5 1.5 %collective-permute-done.5 = f32[24,128]{1,0:T(8,128)S(1)} collective-permute-done((f32[24,128]{1,0:T(8,128)S(1)}, f32[24,128]{1,0:T(8,128)S(1)}, u32[]{:S(2)}, u32[]{:S(2)}) %collective-permute-start.5) | collective-permute-done | bytes 12320 | tf_op jit(solution)/shard_map/ppermute | solution.py:330
  33.0 4.3 %collective-permute-start.7 = (f32[72,128]{1,0:T(8,128)S(1)}, f32[72,128]{1,0:T(8,128)S(1)}, u32[]{:S(2)}, u32[]{:S(2)}) collective-permute-start(f32[72,128]{1,0:T(8,128)S(1)} %constant_dynamic-update-slice_fusion.own), channel_id=1, source_target_pairs={{1,2},{2,1},{3,4},{4,3},{5,6},{6,5},{7,8},{8,7},{9,10},{10,9},{11,... | collective-permute-start | bytes 110600 | tf_op jit(solution)/shard_map/ppermute | solution.py:330
  37.3 0.1 collective-permute-start.6
  37.4 3.5 %collective-permute-done.7.side_b = f32[72,128]{1,0:T(8,128)S(1)} collective-permute-done((f32[72,128]{1,0:T(8,128)S(1)}, f32[72,128]{1,0:T(8,128)S(1)}, u32[]{:S(2)}, u32[]{:S(2)}) %collective-permute-start.7) | collective-permute-done | bytes 36896 | tf_op jit(solution)/shard_map/ppermute | solution.py:330
  40.9 0.4 collective-permute-done.6.side_a
  41.4 9.0 %first.1 = (f32[3,32,80,128]{3,2,1,0:T(8,128)S(1)}, f32[24,128]{1,0:T(8,128)S(1)}) custom-call(s32[2]{0:T(128)S(1)} %pad_add_fusion.par, s32[2,24]{1,0:T(2,128)S(1)} %copy-done.5, s32[2,24]{1,0:T(2,128)S(1)} %copy-done.6, f32[72,128]{1,0:T(8,128)S(1)} %constant_dynamic-update-slice_fusion.own, f32[72,128]{1,0:T(8,128)S(1)} %collective-permute-done.6.side_a, ...), custom_call_target="tpu_custom_call" | custom-call | tf_op jit(solution)/shard_map/first/pallas_call | solution.py:315
  50.4 1.9 %collective-permute-start.9 = (f32[24,128]{1,0:T(8,128)S(1)}, f32[24,128]{1,0:T(8,128)S(1)}, u32[]{:S(2)}, u32[]{:S(2)}) collective-permute-start(f32[24,128]{1,0:T(8,128)S(1)} %get-tuple-element.21), channel_id=1, source_target_pairs={{16,32},{32,16},{48,64},{64,48},{80,96},{96,80},{112,128},{128,112... | collective-permute-start | bytes 36872 | tf_op jit(solution)/shard_map/ppermute | solution.py:330
  52.3 0.8 %collective-permute-start.8 = (f32[24,128]{1,0:T(8,128)S(1)}, f32[24,128]{1,0:T(8,128)S(1)}, u32[]{:S(2)}, u32[]{:S(2)}) collective-permute-start(f32[24,128]{1,0:T(8,128)S(1)} %get-tuple-element.21), channel_id=1, source_target_pairs={{0,16},{16,0},{32,48},{48,32},{64,80},{80,64},{96,112},{112,96},{1... | collective-permute-start | bytes 36872 | tf_op jit(solution)/shard_map/ppermute | solution.py:330
  53.1 0.8 %collective-permute-done.8 = f32[24,128]{1,0:T(8,128)S(1)} collective-permute-done((f32[24,128]{1,0:T(8,128)S(1)}, f32[24,128]{1,0:T(8,128)S(1)}, u32[]{:S(2)}, u32[]{:S(2)}) %collective-permute-start.8) | collective-permute-done | bytes 12320 | tf_op jit(solution)/shard_map/ppermute | solution.py:330
  53.9 2.7 %collective-permute-done.9 = f32[24,128]{1,0:T(8,128)S(1)} collective-permute-done((f32[24,128]{1,0:T(8,128)S(1)}, f32[24,128]{1,0:T(8,128)S(1)}, u32[]{:S(2)}, u32[]{:S(2)}) %collective-permute-start.9) | collective-permute-done | bytes 12320 | tf_op jit(solution)/shard_map/ppermute | solution.py:330
  56.6 3.9 %collective-permute-start.11 = (f32[72,128]{1,0:T(8,128)S(1)}, f32[72,128]{1,0:T(8,128)S(1)}, u32[]{:S(2)}, u32[]{:S(2)}) collective-permute-start(f32[72,128]{1,0:T(8,128)S(1)} %constant_dynamic-update-slice_fusion.3.own), channel_id=1, source_target_pairs={{1,2},{2,1},{3,4},{4,3},{5,6},{6,5},{7,8},{8,7},{9,10},{10,9},{11,... | collective-permute-start | bytes 110600 | tf_op jit(solution)/shard_map/ppermute | solution.py:330
  60.5 0.1 collective-permute-start.10
  60.6 3.9 %collective-permute-done.11.side_b = f32[72,128]{1,0:T(8,128)S(1)} collective-permute-done((f32[72,128]{1,0:T(8,128)S(1)}, f32[72,128]{1,0:T(8,128)S(1)}, u32[]{:S(2)}, u32[]{:S(2)}) %collective-permute-start.11) | collective-permute-done | bytes 36896 | tf_op jit(solution)/shard_map/ppermute | solution.py:330
  64.5 9.5 %second.1 = f32[3,80,32,128]{3,2,1,0:T(8,128)} custom-call(s32[2]{0:T(128)S(1)} %pad_add_fusion.par, f32[72,128]{1,0:T(8,128)S(1)} %constant_dynamic-update-slice_fusion.3.own, f32[72,128]{1,0:T(8,128)S(1)} %collective-permute-done.10.side_a, f32[72,128]{1,0:T(8,128)S(1)} %collective-permute-done.11.side_b, f32[3,32,80,128]{3,2,1,0:T(8,128)S(1)} %get-tuple-element.22.state), custom_call_target="tpu_custom_call" | custom-call | tf_op jit(solution)/shard_map/second/pallas_call | solution.py:315
  (32 shorter events, 0.1 us)
Async XLA Ops:
  0.0 15.4 %copy-start.8 = (s32[2,24]{1,0:T(2,128)S(1)}, s32[2,24]{1,0:T(2,128)}, u32[]{:S(2)}) copy-start(s32[2,24]{1,0:T(2,128)} %param.16) | copy-start | bytes 580
  0.0 15.5 %copy-start.9 = (f32[2,24]{1,0:T(2,128)S(1)}, f32[2,24]{1,0:T(2,128)}, u32[]{:S(2)}) copy-start(f32[2,24]{1,0:T(2,128)} %param.12) | copy-start | bytes 580
  0.0 15.5 %copy-start.7 = (s32[2,24,9]{1,0,2:T(2,128)S(1)}, s32[2,24,9]{1,0,2:T(2,128)}, u32[]{:S(2)}) copy-start(s32[2,24,9]{1,0,2:T(2,128)} %param.17) | copy-start | bytes 5188
  0.0 15.7 %copy-start.10 = (f32[2,24]{1,0:T(2,128)S(1)}, f32[2,24]{1,0:T(2,128)}, u32[]{:S(2)}) copy-start(f32[2,24]{1,0:T(2,128)} %param.13) | copy-start | bytes 580
  0.0 19.2 %copy-start.6 = (s32[2,24]{1,0:T(2,128)S(1)}, s32[2,24]{1,0:T(2,128)}, u32[]{:S(2)}) copy-start(s32[2,24]{1,0:T(2,128)} %kind.3) | copy-start | bytes 580
  0.0 19.2 %copy-start.5 = (s32[2,24]{1,0:T(2,128)S(1)}, s32[2,24]{1,0:T(2,128)}, u32[]{:S(2)}) copy-start(s32[2,24]{1,0:T(2,128)} %cell.3) | copy-start | bytes 580
  0.0 19.2 %copy-start.4 = (f32[1,32,128]{2,1,0:T(8,128)S(1)}, f32[1,32,128]{2,1,0:T(8,128)}, u32[]{:S(2)}) copy-start(f32[1,32,128]{2,1,0:T(8,128)} %cr.1) | copy-start | bytes 49156
  0.0 19.2 %copy-start.3 = (f32[1,32,128]{2,1,0:T(8,128)S(1)}, f32[1,32,128]{2,1,0:T(8,128)}, u32[]{:S(2)}) copy-start(f32[1,32,128]{2,1,0:T(8,128)} %cc.1) | copy-start | bytes 49156
  0.2 2.1 %copy-start = (f32[3,80,32,128]{3,2,1,0:T(8,128)S(1)}, f32[3,80,32,128]{3,2,1,0:T(8,128)}, u32[]{:S(2)}) copy-start(f32[3,80,32,128]{3,2,1,0:T(8,128)} %x_hbm.1) | copy-start | bytes 11796484
  5.4 1.9 %copy-start.1 = (f32[3,32,80,128]{3,2,1,0:T(8,128)}, f32[3,32,80,128]{3,2,1,0:T(8,128)S(1)}, u32[]{:S(2)}) copy-start(f32[3,32,80,128]{3,2,1,0:T(8,128)S(1)} %get-tuple-element.14.xt) | copy-start | bytes 11796484
  7.3 11.9 %collective-permute-start = (f32[3,80,128]{2,1,0:T(8,128)S(1)}, f32[3,80,128]{2,1,0:T(8,128)S(1)}, u32[]{:S(2)}, u32[]{:S(2)}) collective-permute-start(f32[3,80,128]{2,1,0:T(8,128)S(1)} %get-tuple-element.15), channel_id=1, source_target_pairs={{0,16},{16,0},{32,48},{48,32},{64,80},{80,64},{96,112},{112,96},{1... | collective-permute-start | bytes 368648 | tf_op jit(solution)/shard_map/ppermute | solution.py:330
  7.3 11.9 %collective-permute-start.1 = (f32[3,80,128]{2,1,0:T(8,128)S(1)}, f32[3,80,128]{2,1,0:T(8,128)S(1)}, u32[]{:S(2)}, u32[]{:S(2)}) collective-permute-start(f32[3,80,128]{2,1,0:T(8,128)S(1)} %get-tuple-element.16), channel_id=1, source_target_pairs={{16,32},{32,16},{48,64},{64,48},{80,96},{96,80},{112,128},{128,112... | collective-permute-start | bytes 368648 | tf_op jit(solution)/shard_map/ppermute | solution.py:330
  9.4 6.3 %collective-permute-start.2 = (f32[80,128]{1,0:T(8,128)S(1)}, f32[80,128]{1,0:T(8,128)S(1)}, u32[]{:S(2)}, u32[]{:S(2)}) collective-permute-start(f32[80,128]{1,0:T(8,128)S(1)} %get-tuple-element.17), channel_id=1, source_target_pairs={{0,1},{1,0},{2,3},{3,2},{4,5},{5,4},{6,7},{7,6},{8,9},{9,8},{10,11... | collective-permute-start | bytes 122888 | tf_op jit(solution)/shard_map/ppermute | solution.py:330
  11.1 8.1 %collective-permute-start.3 = (f32[80,128]{1,0:T(8,128)S(1)}, f32[80,128]{1,0:T(8,128)S(1)}, u32[]{:S(2)}, u32[]{:S(2)}) collective-permute-start(f32[80,128]{1,0:T(8,128)S(1)} %get-tuple-element.18), channel_id=1, source_target_pairs={{1,2},{2,1},{3,4},{4,3},{5,6},{6,5},{7,8},{8,7},{9,10},{10,9},{11,... | collective-permute-start | bytes 122888 | tf_op jit(solution)/shard_map/ppermute | solution.py:330
  19.2 2.1 %copy-start.2 = (f32[3,32,80,128]{3,2,1,0:T(8,128)S(1)}, f32[3,32,80,128]{3,2,1,0:T(8,128)}, u32[]{:S(2)}) copy-start(f32[3,32,80,128]{3,2,1,0:T(8,128)} %copy-done.1) | copy-start | bytes 11796484
  26.8 6.2 %collective-permute-start.5 = (f32[24,128]{1,0:T(8,128)S(1)}, f32[24,128]{1,0:T(8,128)S(1)}, u32[]{:S(2)}, u32[]{:S(2)}) collective-permute-start(f32[24,128]{1,0:T(8,128)S(1)} %get-tuple-element.19), channel_id=1, source_target_pairs={{16,32},{32,16},{48,64},{64,48},{80,96},{96,80},{112,128},{128,112... | collective-permute-start | bytes 36872 | tf_op jit(solution)/shard_map/ppermute | solution.py:330
  29.9 1.6 %collective-permute-start.4 = (f32[24,128]{1,0:T(8,128)S(1)}, f32[24,128]{1,0:T(8,128)S(1)}, u32[]{:S(2)}, u32[]{:S(2)}) collective-permute-start(f32[24,128]{1,0:T(8,128)S(1)} %get-tuple-element.19), channel_id=1, source_target_pairs={{0,16},{16,0},{32,48},{48,32},{64,80},{80,64},{96,112},{112,96},{1... | collective-permute-start | bytes 36872 | tf_op jit(solution)/shard_map/ppermute | solution.py:330
  33.0 8.0 %collective-permute-start.7 = (f32[72,128]{1,0:T(8,128)S(1)}, f32[72,128]{1,0:T(8,128)S(1)}, u32[]{:S(2)}, u32[]{:S(2)}) collective-permute-start(f32[72,128]{1,0:T(8,128)S(1)} %constant_dynamic-update-slice_fusion.own), channel_id=1, source_target_pairs={{1,2},{2,1},{3,4},{4,3},{5,6},{6,5},{7,8},{8,7},{9,10},{10,9},{11,... | collective-permute-start | bytes 110600 | tf_op jit(solution)/shard_map/ppermute | solution.py:330
  37.3 4.0 %collective-permute-start.6 = (f32[72,128]{1,0:T(8,128)S(1)}, f32[72,128]{1,0:T(8,128)S(1)}, u32[]{:S(2)}, u32[]{:S(2)}) collective-permute-start(f32[72,128]{1,0:T(8,128)S(1)} %constant_dynamic-update-slice_fusion.own), channel_id=1, source_target_pairs={{0,1},{1,0},{2,3},{3,2},{4,5},{5,4},{6,7},{7,6},{8,9},{9,8},{10,11... | collective-permute-start | bytes 110600 | tf_op jit(solution)/shard_map/ppermute | solution.py:330
  50.4 6.2 %collective-permute-start.9 = (f32[24,128]{1,0:T(8,128)S(1)}, f32[24,128]{1,0:T(8,128)S(1)}, u32[]{:S(2)}, u32[]{:S(2)}) collective-permute-start(f32[24,128]{1,0:T(8,128)S(1)} %get-tuple-element.21), channel_id=1, source_target_pairs={{16,32},{32,16},{48,64},{64,48},{80,96},{96,80},{112,128},{128,112... | collective-permute-start | bytes 36872 | tf_op jit(solution)/shard_map/ppermute | solution.py:330
  52.3 1.6 %collective-permute-start.8 = (f32[24,128]{1,0:T(8,128)S(1)}, f32[24,128]{1,0:T(8,128)S(1)}, u32[]{:S(2)}, u32[]{:S(2)}) collective-permute-start(f32[24,128]{1,0:T(8,128)S(1)} %get-tuple-element.21), channel_id=1, source_target_pairs={{0,16},{16,0},{32,48},{48,32},{64,80},{80,64},{96,112},{112,96},{1... | collective-permute-start | bytes 36872 | tf_op jit(solution)/shard_map/ppermute | solution.py:330
  56.6 8.0 %collective-permute-start.11 = (f32[72,128]{1,0:T(8,128)S(1)}, f32[72,128]{1,0:T(8,128)S(1)}, u32[]{:S(2)}, u32[]{:S(2)}) collective-permute-start(f32[72,128]{1,0:T(8,128)S(1)} %constant_dynamic-update-slice_fusion.3.own), channel_id=1, source_target_pairs={{1,2},{2,1},{3,4},{4,3},{5,6},{6,5},{7,8},{8,7},{9,10},{10,9},{11,... | collective-permute-start | bytes 110600 | tf_op jit(solution)/shard_map/ppermute | solution.py:330
  60.5 4.0 %collective-permute-start.10 = (f32[72,128]{1,0:T(8,128)S(1)}, f32[72,128]{1,0:T(8,128)S(1)}, u32[]{:S(2)}, u32[]{:S(2)}) collective-permute-start(f32[72,128]{1,0:T(8,128)S(1)} %constant_dynamic-update-slice_fusion.3.own), channel_id=1, source_target_pairs={{0,1},{1,0},{2,3},{3,2},{4,5},{5,4},{6,7},{7,6},{8,9},{9,8},{10,11... | collective-permute-start | bytes 110600 | tf_op jit(solution)/shard_map/ppermute | solution.py:330
where the time goes:
time: 74.3 us; the launch traced here: 74 us
  Pallas kernels  27 us (36%)
  starting transfers between devices  23.2 us (31%)
  waiting for transfers between devices  17.2 us (23%)
  local copies, waits for them, and re-layouts  6.37 us (9%)
    pallas_call x4, Pallas kernels, call(): pl.pallas_call(kernel, out_shape=outs, in_specs=[spec(s) for s in spaces]...  27 us
    ppermute x12, starting transfers between devices, swap(): return lax.ppermute(x, axis, pairs)  23.2 us
    ppermute x12, waiting for transfers between devices, swap(): return lax.ppermute(x, axis, pairs)  17.2 us
    unnamed x27, local copies, waits for them, and re-layouts  6.27 us
  transfers between devices with their start and end apart: 12, of which 8 were waited for; matrix products, arithmetic and copies ran while one was open for 0% of the time, Pallas kernels for 0%

commit v1 on v0

v1 whole, which is shorter than its diff:
```python
import jax
import jax.numpy as jnp
from jax import lax
from jax.experimental import pallas as pl
from jax.experimental.pallas import tpu as pltpu
from jax.sharding import PartitionSpec as P

F, M, R, C, K = 3, 80, 32, 128, 24
GAIN, INNOV, ALPHA, ROW, COL, KIND = 80, 81, 82, 83, 84, 85
AE, AW, AN, AS, LIST, T = 88, 89, 90, 91, 96, 112
VALUE, ERROR, LIVE = GAIN, INNOV, ALPHA
LATER = 96
S = 80
f32, bf16 = jnp.float32, jnp.bfloat16
VMEM = pltpu.VMEM
MiB = 1 << 20


def lanes(shape):
    return lax.broadcasted_iota(jnp.int32, shape, len(shape) - 1)


def split(x):
    hi = x.astype(bf16)
    return hi, (x - hi.astype(f32)).astype(bf16)


def split3(x):
    hi = x.astype(bf16)
    rest = x - hi.astype(f32)
    mid = rest.astype(bf16)
    return hi, mid, (rest - mid.astype(f32)).astype(bf16)


def dot(a, b, dims=((1,), (0,))):
    return lax.dot_general(a, b, (dims, ((), ())), preferred_element_type=f32)


def subs(shape):
    return lax.broadcasted_iota(jnp.int32, shape, 0)


def parity(axis):
    return lax.rem(lax.axis_index(axis), 2)


def flag(value, shape):
    return (jnp.zeros(shape, jnp.int32) + value) == 1


def stencil(u, v):
    uu, vv = 0.5 * u * u, 0.5 * v * v
    return 1.0 - 2.0 * uu - 2.0 * vv, uu - 0.5 * u, uu + 0.5 * u, vv - 0.5 * v, vv + 0.5 * v


def own_part(b, start, xt, cell, kind, cc, cr, value, error, live, listed, part):
    lane, lane1 = lanes((M, C)), lanes((1, C))
    zero = jnp.zeros((1, C), f32)
    prior = jnp.zeros((M, C), f32)
    rows = [zero] * 7
    for s in range(K):
        at = cell[b, s]
        r, c = at // C, at % C
        f = kind[b, s]
        rf = zero + r.astype(f32)
        here, ae, aw, an, as_ = stencil(cc[0, pl.ds(r, 1), :], cr[0, pl.ds(r, 1), :])
        turn = lax.rem(start + s + C - c, C)
        fields = [rf, zero + c.astype(f32), zero + f.astype(f32)]
        fields += [pltpu.roll(w, turn, 1) for w in (ae, aw, an, as_)]
        mine1 = lane1 == start + s
        rows = [jnp.where(mine1, w, old) for w, old in zip(fields, rows)]
        ae = jnp.where(lane1 == C - 1, 0.0, ae)
        aw = jnp.where(lane1 == 0, 0.0, aw)
        an = jnp.where(rf == R - 1.0, 0.0, an)
        as_ = jnp.where(rf == 0.0, 0.0, as_)
        x = xt[f, r]
        y = here * x + ae * pltpu.roll(x, C - 1, 1) + aw * pltpu.roll(x, 1, 1)
        y = y + an * xt[f, jnp.minimum(r + 1, R - 1)] + as_ * xt[f, jnp.maximum(r - 1, 0)]
        prior = jnp.where(lane == start + s, pltpu.roll(y, turn, 1), prior)
    part[...] = jnp.zeros((T, C), f32)
    part[:M] = prior
    for n, w in zip((ROW, COL, KIND, AE, AW, AN, AS), rows):
        part[n : n + 1, :] = w
    keep = slice(start, start + K)
    part[VALUE : VALUE + 1, keep] = value[b : b + 1, :]
    part[ERROR : ERROR + 1, keep] = error[b : b + 1, :]
    part[LIVE : LIVE + 1, keep] = live[b : b + 1, :].astype(f32)
    for n in range(9):
        part[LIST + n : LIST + n + 1, keep] = listed[n, b : b + 1, :].astype(f32)


def small_copies(srcs, dsts, sems):
    return [pltpu.make_async_copy(a, b, sems.at[n]) for n, (a, b) in enumerate(zip(srcs, dsts))]


def edges_kernel(*refs):
    x_hbm, small = refs[0], refs[1:9]
    xt, pay_a, pay_b = refs[9:12]
    here = refs[12:20]
    buf, acc, sem, small_sem = refs[20:]
    for ib in range(R // 8):
        for f in range(F):
            pltpu.make_async_copy(
                x_hbm.at[f, :, pl.ds(ib * 8, 8), :], buf.at[ib, f], sem.at[ib, f]
            ).start()
    copies = small_copies(small, here, small_sem)
    for c in copies:
        c.start()
    acc[...] = jnp.zeros_like(acc)
    lane = lanes((M, C))
    for ib in range(R // 8):
        for f in range(F):
            pltpu.make_async_copy(
                x_hbm.at[f, :, pl.ds(ib * 8, 8), :], buf.at[ib, f], sem.at[ib, f]
            ).wait()
            rows = buf.at[ib, f].reshape(M * 8, C)
            first, last = acc[0, :M], acc[1, :M]
            for r in range(8):
                v = rows[pl.ds(r, M, stride=8), :]
                i = ib * 8 + r
                k = f * R + i
                xt[f, i] = v
                turned = pltpu.roll(v, k, 1) if k else v
                first = jnp.where(lane == k, turned, first)
                last = jnp.where(lane == (k - 1) % C, turned, last)
            acc[0, :M] = first
            acc[1, :M] = last
    first, last = acc[0, :M], pltpu.roll(acc[1, :M], 1, 1)
    ra = jnp.where(parity("lat") == 1, 0, R - 1)
    rb = R - 1 - ra
    for f in range(F):
        pay_a[pl.ds(f * M, M), :] = xt[f, ra]
        pay_b[pl.ds(f * M, M), :] = xt[f, rb]
    for pay in (pay_a, pay_b):
        pay[pl.ds(F * M, M), :] = first
        pay[pl.ds(F * M + M, M), :] = last
    for c in copies:
        c.wait()
    part = acc.at[2]
    own_part(0, 0, xt, *here, part)
    pay_a[pl.ds(5 * M, T), :] = part[...]
    pay_b[pl.ds(5 * M, T), :] = part[...]


def later_kernel(*refs):
    xt, small, out, here, small_sem = refs[0], refs[1:9], refs[9], refs[10:18], refs[18]
    copies = small_copies(small, here, small_sem)
    for c in copies:
        c.start()
    for c in copies:
        c.wait()
    own_part(1, LATER, xt, *here, out)


def combine(own, a, b):
    few = lanes((T, C)) < K
    return (
        own
        + pltpu.roll(jnp.where(few, a, 0.0), K, 1)
        + pltpu.roll(jnp.where(few, b, 0.0), 2 * K, 1)
    )


def lane_group():
    lane = lanes((1, C))
    group = jnp.where(lane < 2 * K, 1, jnp.where(lane < 3 * K, 2, 3))
    return jnp.where((lane < K) | ((lane >= LATER) & (lane < LATER + K)), 0, group)


def pickup(sources, key):
    hot = (subs((F * C, C)).astype(f32) == key).astype(f32).astype(bf16)
    return sum(dot(h, hot) for h in split3(jnp.concatenate(sources, axis=1)))


def rows_kernel(xt, pay, later, got_a, got_b, out_a, out_b):
    pa, pb = parity("lat"), parity("lon")
    base = 5 * M
    comb = combine(pay[pl.ds(base, T), :], got_a[pl.ds(base, T), :], got_b[pl.ds(base, T), :])
    comb = comb + later[...]
    row, col, kind = comb[ROW : ROW + 1], comb[COL : COL + 1], comb[KIND : KIND + 1]
    group = lane_group()
    edge_a = jnp.where(pa == 1, 0, R - 1)
    edge_b = R - 1 - edge_a
    cellkey = kind * C + col

    def key(n, edge):
        return jnp.where((group == n) & (row == edge.astype(f32)), cellkey, -1.0)

    total = pickup([got_a[pl.ds(f * M, M), :] for f in range(F)], key(0, edge_a))
    total += pickup([got_b[pl.ds(f * M, M), :] for f in range(F)], key(0, edge_b))
    total += pickup([xt[f, edge_a] for f in range(F)], key(1, edge_b))
    total += pickup([xt[f, edge_b] for f in range(F)], key(2, edge_a))
    coef = jnp.where(row == 0.0, comb[AS : AS + 1], comb[AN : AN + 1])
    prior = comb[:M] + coef * total
    odd = flag(pb, (M, C))
    for n, src in enumerate((pay, got_a, got_b)):
        first, last = src[pl.ds(F * M, M), :], src[pl.ds(F * M + M, M), :]
        out_a[pl.ds(n * M, M), :] = jnp.where(odd, first, last)
        out_b[pl.ds(n * M, M), :] = jnp.where(odd, last, first)
    for out in (out_a, out_b):
        out[pl.ds(3 * M, M), :] = prior
        out[pl.ds(4 * M, T - M), :] = comb[M:]


def statistics(t):
    prior = t[:M]
    ybar = jnp.sum(prior, axis=0, keepdims=True) / M
    yp = prior - ybar
    spread = jnp.sum(yp * yp, axis=0, keepdims=True) / (M - 1)
    err = t[ERROR : ERROR + 1]
    total = spread + err
    total = jnp.where(total == 0.0, 1.0, total)
    gain = t[LIVE : LIVE + 1] / total
    alpha = 1.0 / (1.0 + jnp.sqrt(err / total))
    innov = t[VALUE : VALUE + 1] - ybar
    return yp, gain, innov, alpha


def stack_fields(yp, rows):
    sub = subs((16, C))
    extra = jnp.zeros((16, C), f32)
    for n, v in enumerate(rows):
        extra = jnp.where(sub == n, v, extra)
    return jnp.concatenate([yp, extra], axis=0)


def choose(index, raw, yp, gain, innov, alpha):
    sa = 1 - 2 * parity("lat")
    sb = 1 - 2 * parity("lon")
    db = (0, sb, -sb)[index]
    group = lane_group()
    chosen = jnp.zeros((1, C), f32)
    row = raw[ROW : ROW + 1, :]
    for n, da in enumerate((0, sa, -sa)):
        listed = raw[pl.ds(LIST + (1 - da) * 3 + (1 - db), 1), :]
        chosen = jnp.where(group == n, listed, chosen)
        row = jnp.where(group == n, row + jnp.asarray(da * R, f32), row)
    col = raw[COL : COL + 1, :] + jnp.asarray(db * C, f32)
    factor = gain * chosen
    near = (row > -float(R)) & (row < 2.0 * R - 1.0) & (col > -float(R)) & (col < C + R - 1.0)
    act = near & (factor != 0.0) & (lanes((1, C)) < 3 * K)
    return stack_fields(yp, (factor, innov, alpha, row, col)), jnp.where(act, 1.0, 0.0)


def ranks(actives):
    before = (subs((C, C)) < lanes((C, C))).astype(f32).astype(bf16)
    out, offset = [], jnp.zeros((1, 1), f32)
    for act in actives:
        r = dot(jnp.broadcast_to(act, (8, C)).astype(bf16), before)[:1] + offset
        out.append(jnp.where(act > 0.0, r, -1.0))
        offset = offset + jnp.sum(act, axis=1, keepdims=True)
    return out, sum(jnp.sum(a) for a in actives).astype(jnp.int32)


def spread_lanes(hi, lo):
    r = lax.broadcasted_iota(jnp.int32, (C, 2 * C), 0)
    c = lax.broadcasted_iota(jnp.int32, (C, 2 * C), 1)
    keep = r < S
    e_hi = (((c == r) | (c == r + 2 * S)) & keep).astype(f32).astype(bf16)
    e_lo = ((c == r + S) & keep).astype(f32).astype(bf16)
    return (dot(hi, e_hi) + dot(lo, e_lo)).astype(bf16)


def compact(fields, rank, chunk, ycat, bcat, locs):
    p = subs((C, F * C)).astype(f32) + jnp.asarray(chunk * S, f32)
    own = subs((C, F * C)) < S
    pick = ((rank == p) & own).astype(f32).astype(bf16)
    turned = sum(dot(t, pick, ((1,), (1,))) for t in split3(fields))
    chosen = jnp.concatenate([turned, jnp.zeros((32, C), f32)], axis=0).T[:S]
    ycat[chunk] = spread_lanes(*split(chosen))
    back = turned[INNOV : INNOV + 1, :] - turned[ALPHA : ALPHA + 1, :] * turned[:M]
    bcat[chunk] = spread_lanes(*split(back))
    locs[chunk, 0] = jnp.broadcast_to(chosen[:, ROW : ROW + 1], (S, C))
    locs[chunk, 1] = jnp.broadcast_to(chosen[:, COL : COL + 1], (S, C))
    locs[chunk, 2] = jnp.broadcast_to(chosen[:, GAIN : GAIN + 1], (S, C)) / (M - 1)


def compact_all(fields, rank, count, ycat, bcat, locs):
    compact(fields, rank, 0, ycat, bcat, locs)

    @pl.when(count > S)
    def _():
        def body(j, carry):
            compact(fields, rank, j, ycat, bcat, locs)
            return carry

        lax.fori_loop(1, (count + S - 1) // S, body, 0)


def taper(d):
    z = jnp.maximum(0.0, 1.0 - jnp.abs(d) / R)
    return z * z


def update(p, lw, ycat, bcat):
    hi, lo = split(p)
    none = jnp.zeros((2 * C - 3 * M, p.shape[1]), bf16)
    proj = dot(ycat, jnp.concatenate([hi, hi, lo, none], axis=0))
    hi, lo = split(proj * lw)
    return dot(bcat, jnp.concatenate([hi, hi, lo, none], axis=0))


def tables_kernel(pay, got_a, got_b, own_in, got_x, got_y, after, table, count_out, ycat, bcat, locs):
    pb = parity("lon")
    edge_x = jnp.where(pb == 1, 0.0, C - 1.0)
    edge_y = C - 1.0 - edge_x
    group = lane_group()
    odd = flag(pb, (M, C))
    mine_x, mine_y = [], []
    for src in (pay, got_a, got_b):
        first, last = src[pl.ds(F * M, M), :], src[pl.ds(F * M + M, M), :]
        mine_x.append(jnp.where(odd, first, last))
        mine_y.append(jnp.where(odd, last, first))

    def complete(t, parts):
        row, col, kind = t[ROW : ROW + 1], t[COL : COL + 1], t[KIND : KIND + 1]
        at = group.astype(f32) * C + kind * R + row
        total = jnp.zeros((M, C), f32)
        for packs, edge in parts:
            total += pickup(packs, jnp.where((group < 3) & (col == edge), at, -1.0))
        coef = jnp.where(col == 0.0, t[AW : AW + 1], t[AE : AE + 1])
        return t[:M] + coef * total

    def packs(got):
        return [got[pl.ds(n * M, M), :] for n in range(3)]

    base = 3 * M
    out = []
    later = None
    for index, (src, parts) in enumerate((
        (own_in, ((packs(got_x), edge_x), (packs(got_y), edge_y))),
        (got_x, ((mine_x, edge_y),)),
        (got_y, ((mine_y, edge_x),)),
    )):
        raw = src.at[pl.ds(base, T), :]
        t = raw[...]
        whole = jnp.concatenate([complete(t, parts), t[M:]], axis=0)
        if index == 0:
            later = whole
        out.append(choose(index, raw, *statistics(whole)))
    fields = jnp.concatenate([a for a, _ in out], axis=1)
    rank, count = ranks([a for _, a in out])
    rank = jnp.concatenate(rank, axis=1)
    count_out[0] = count
    compact_all(fields, rank, count, ycat, bcat, locs)

    prior = later[:M]
    row, col = later[ROW : ROW + 1], later[COL : COL + 1]

    def point(j, add):
        lw = taper(locs[j, 0] - row) * taper(locs[j, 1] - col) * locs[j, 2]
        return add + update(prior, lw, ycat[j], bcat[j])

    add = lax.fori_loop(0, jnp.maximum((count + S - 1) // S, 1), point, jnp.zeros((M, C), f32))
    later = jnp.concatenate([prior + add, later[M:]], axis=0)
    yp, gain, innov, alpha = statistics(later)
    fresh = stack_fields(yp, (gain, innov, alpha, row, col))
    fresh = jnp.concatenate([fresh, later[LIST:]], axis=0)
    lane = lanes((T, C))
    fresh = jnp.where((lane >= LATER) & (lane < LATER + K), fresh, 0.0)
    table[...] = pltpu.roll(fresh, C - LATER, 1)


def combine_kernel(own, a, b, out):
    out[...] = combine(own[...], a[...], b[...])


def advect_kernel(xt, got_a, got_b, cc_hbm, cr_hbm, state, edge, cc, cr, sems):
    copies = small_copies((cc_hbm, cr_hbm), (cc, cr), sems)
    for c in copies:
        c.start()
    for c in copies:
        c.wait()
    lane1 = lanes((1, C))
    odd_a = flag(parity("lat"), (M, C))

    def one(i, low, high):
        here, ae, aw, an, as_ = stencil(cc[0, pl.ds(i, 1), :], cr[0, pl.ds(i, 1), :])
        edge[pl.ds(i, 1), :] = jnp.where(
            lane1 == 0, aw, jnp.where(lane1 == C - 1, ae, 0.0)
        )
        ae = jnp.where(lane1 == C - 1, 0.0, ae)
        aw = jnp.where(lane1 == 0, 0.0, aw)
        for f in range(F):
            x = xt[f, i]
            ha, hb = got_a[pl.ds(f * M, M), :], got_b[pl.ds(f * M, M), :]
            xs = jnp.where(odd_a, ha, hb) if low else xt[f, i - 1]
            xn = jnp.where(odd_a, hb, ha) if high else xt[f, i + 1]
            y = here * x + ae * pltpu.roll(x, C - 1, 1) + aw * pltpu.roll(x, 1, 1)
            state[f, i] = y + an * xn + as_ * xs

    one(0, True, False)
    one(R - 1, False, True)

    def body(n, carry):
        one(2 * n + 1, False, False)
        one(2 * n + 2, False, False)
        return carry

    lax.fori_loop(0, R // 2 - 1, body, 0)


def lay_halos(got_x, got_y, merged):
    odd_lane = (lanes((M, C)) % 2) == 1
    odd_b = flag(parity("lon"), (M, C))
    got_1, got_2 = got_x[pl.ds(0, M), :], got_y[pl.ds(0, M), :]
    east = pltpu.roll(jnp.where(odd_b, got_2, got_1), C - 1, 1)
    west = jnp.where(odd_b, got_1, got_2)
    merged[0] = jnp.where(odd_lane, east, west)
    merged[1] = jnp.where(odd_lane, west, east)


def sweeps(row_of, count, ycat, bcat, locs, col_w, total, emit):
    def weigh(j):
        col_w[...] = taper(locs[j, 1] - lanes((S, C)).astype(f32)) * locs[j, 2]

    def sweep(base, j, put):
        def local(i):
            return taper(locs[j, 0] - i.astype(f32)) * col_w[...]

        def body(n, carry):
            i = 2 * n
            lw = jnp.concatenate([local(i), local(i + 1)], axis=1)
            for f in range(F):
                pair = row_of(f, i, 0), row_of(f, i + 1, 1)
                d = update(jnp.concatenate(pair, axis=1), lw, ycat[j], bcat[j])
                if base is not None:
                    pair = base[f, i], base[f, i + 1]
                put(n, f, pair[0] + d[:, :C], pair[1] + d[:, C:])
            return carry

        return body

    def keep(n, f, a, b):
        total[f, 2 * n] = a
        total[f, 2 * n + 1] = b

    @pl.when(count > S)
    def _():
        weigh(1)
        lax.fori_loop(0, R // 2, sweep(None, 1, keep), 0)

        @pl.when(count > 2 * S)
        def _():
            weigh(2)
            lax.fori_loop(0, R // 2, sweep(total, 2, keep), 0)

        weigh(0)
        emit(sweep, total)

    @pl.when(count <= S)
    def _():
        weigh(0)
        emit(sweep, None)


def first_kernel(count, state, edge, got_x, got_y, ycat, bcat, locs, out, col_w, total, merged):
    lay_halos(got_x, got_y, merged)

    def row_of(f, i, odd):
        halo = pltpu.roll(merged[odd], lax.rem(2 * C - (f * R + i), C), 1)
        return state[f, i] + halo * edge[pl.ds(i, 1), :]

    def emit(sweep, base):
        def put(n, f, a, b):
            out[f, 2 * n] = a
            out[f, 2 * n + 1] = b

        lax.fori_loop(0, R // 2, sweep(base, 0, put), 0)

    sweeps(row_of, count[0], ycat, bcat, locs, col_w, total, emit)


def second_kernel(own, got_x, got_y, state, out, buf, sem, ycat, bcat, locs, col_w, total):
    parts = []
    for index, raw in enumerate((own, got_x, got_y)):
        t = raw[...]
        rows = (t[GAIN : GAIN + 1], t[INNOV : INNOV + 1], t[ALPHA : ALPHA + 1])
        parts.append(choose(index, raw, t[:M], *rows))
    rank, count = ranks([a for _, a in parts])
    fields = jnp.concatenate([a for a, _ in parts], axis=1)
    compact_all(fields, jnp.concatenate(rank, axis=1), count, ycat, bcat, locs)

    def copy(ib, f):
        return pltpu.make_async_copy(
            buf.at[ib, f], out.at[f, :, pl.ds(ib * 8, 8), :], sem.at[ib, f]
        )

    def emit(sweep, base):
        for ib in range(R // 8):

            def put(n, f, a, b):
                rows = buf.at[ib, f].reshape(M * 8, C)
                r = 2 * (n - 4 * ib)
                rows[pl.ds(r, M, stride=8), :] = a
                rows[pl.ds(r + 1, M, stride=8), :] = b

            lax.fori_loop(4 * ib, 4 * ib + 4, sweep(base, 0, put), 0)
            for f in range(F):
                copy(ib, f).start()

    sweeps(lambda f, i, odd: state[f, i], count, ycat, bcat, locs, col_w, total, emit)
    for ib in range(R // 8):
        for f in range(F):
            copy(ib, f).wait()


def call(kernel, outs, args, scratch=(), scalars=0, hbm=(), out_spaces=None, us=2, limit=24):
    spaces = [
        pltpu.SMEM if n < scalars else pltpu.HBM if n in hbm else VMEM for n in range(len(args))
    ]
    args = [
        pltpu.with_memory_space_constraint(a, s) if a.size > 100000 or s == pltpu.HBM else a
        for a, s in zip(args, spaces)
    ]
    out_spaces = out_spaces or [VMEM] * len(outs)
    return pl.pallas_call(
        kernel,
        out_shape=outs,
        in_specs=[pl.BlockSpec(memory_space=s) for s in spaces],
        out_specs=[pl.BlockSpec(memory_space=s) for s in out_spaces],
        scratch_shapes=scratch,
        compiler_params=pltpu.CompilerParams(vmem_limit_bytes=limit * MiB),
        cost_estimate=pl.CostEstimate(flops=0, transcendentals=0, bytes_accessed=us * 3000000),
        name=kernel.__name__,
    )(*args)


def swap(x, axis, shift):
    n = lax.axis_size(axis)
    pairs = [(i, ((i - shift) ^ 1) + shift) for i in range(n)]
    pairs = [(i, j) for i, j in pairs if i >= shift and 0 <= j < n]
    return lax.ppermute(x, axis, pairs)


def on_device(
    ensemble, courant_cols, courant_rows, obs_value, obs_error, obs_cell, obs_kind, obs_live, obs_list
):
    listed = jnp.transpose(obs_list, (2, 0, 1))
    block = VMEM((F, R, M, C), f32)
    sds = jax.ShapeDtypeStruct
    copies = [VMEM((R // 8, F, M, 8, C), f32)]
    sems = pltpu.SemaphoreType.DMA((R // 8, F))

    small = [
        obs_cell, obs_kind, courant_cols, courant_rows, obs_value, obs_error, obs_live, listed
    ]
    held = [(pltpu.SMEM if n < 2 else VMEM)(a.shape, a.dtype) for n, a in enumerate(small)]
    held_sems = pltpu.SemaphoreType.DMA((len(small),))

    pay_shape = sds((5 * M + T, C), f32)
    xt, pay_a, pay_b = call(
        edges_kernel,
        [block, pay_shape, pay_shape],
        [ensemble, *small],
        [*held, *copies, VMEM((3, T, C), f32), sems, held_sems],
        hbm=range(9),
    )
    got_b, got_a = swap(pay_b, "lat", 1), swap(pay_a, "lat", 0)
    later = call(
        later_kernel, [sds((T, C), f32)], [xt, *small], [*held, held_sems], hbm=range(1, 9), us=1
    )[0]
    lon_shape = sds((3 * M + T, C), f32)
    out_a, out_b = call(rows_kernel, [lon_shape] * 2, [xt, pay_a, later, got_a, got_b])
    got_y, got_x = swap(out_b, "lon", 1), swap(out_a, "lon", 0)
    state, edge = call(
        advect_kernel,
        [block, sds((R, C), f32)],
        [xt, got_a, got_b, courant_cols, courant_rows],
        [held[2], held[3], pltpu.SemaphoreType.DMA((2,))],
        hbm=(3, 4),
    )
    chosen = [sds((3, S, 2 * C), bf16), sds((3, M, 2 * C), bf16), sds((3, 3, S, C), f32)]
    table, count, *picked = call(
        tables_kernel,
        [sds((T, C), f32), sds((1,), jnp.int32), *chosen],
        [pay_a, got_a, got_b, out_a, got_x, got_y, edge],
        out_spaces=[VMEM, pltpu.SMEM, VMEM, VMEM, VMEM],
    )
    tab_b, tab_a = swap(table, "lat", 1), swap(table, "lat", 0)
    column = call(combine_kernel, [sds((T, C), f32)], [table, tab_a, tab_b], us=1)[0]
    col_y, col_x = swap(column, "lon", 1), swap(column, "lon", 0)
    work = [VMEM((S, C), f32), VMEM((F, R, M, C), f32)]
    state = call(
        first_kernel,
        [block],
        [count, state, edge, got_x, got_y, *picked],
        work + [VMEM((2, M, C), f32)],
        scalars=1,
        us=4,
    )[0]
    return call(
        second_kernel,
        [sds((F, M, R, C), f32)],
        [column, col_x, col_y, state],
        [*copies, sems]
        + [VMEM((3, S, 2 * C), bf16), VMEM((3, M, 2 * C), bf16), VMEM((3, 3, S, C), f32)]
        + work,
        out_spaces=[pltpu.HBM],
        us=6,
    )[0]


def solution(mesh):
    tiles = P(None, ("lat", "lon"))
    placed = (
        P(None, None, "lat", "lon"),
        P(None, "lat", "lon"),
        P(None, "lat", "lon"),
        tiles,
        tiles,
        tiles,
        tiles,
        tiles,
        P(None, ("lat", "lon"), None),
    )
    return jax.shard_map(
        on_device,
        mesh=mesh,
        in_specs=placed,
        out_specs=P(None, None, "lat", "lon"),
        check_vma=False,
    )
```

time: 74.3 us -> 56.2 us (0.76)
  the two profiles are of different devices: /device:TPU:134 before, /device:TPU:111 now
where the time goes in v1:
time: 56.2 us; the launch traced here: 55.7 us
  Pallas kernels  31 us (55%)
  starting transfers between devices  20.6 us (37%)
  waiting for transfers between devices  3.93 us (7%)
    pallas_call x8, Pallas kernels, call(): pl.pallas_call(kernel, out_shape=outs, in_specs=[pl.BlockSpec(memory_spac...  31 us
    ppermute x8, starting transfers between devices, swap(): return lax.ppermute(x, axis, pairs)  20.6 us
    ppermute x8, waiting for transfers between devices, swap(): return lax.ppermute(x, axis, pairs)  3.93 us
  transfers between devices with their start and end apart: 8, of which 3 were waited for; matrix products, arithmetic and copies ran while one was open for 0% of the time, Pallas kernels for 28%

profile of v1, /device:TPU:111, one launch (start us, length us, event | category | flops | bytes accessed | tf_op | source)
XLA Modules:
  0.0 55.7 jit_solution(1092291222608315722)
XLA Ops:
  0.0 5.4 %edges_kernel.1 = (f32[3,32,80,128]{3,2,1,0:T(8,128)S(1)}, f32[512,128]{1,0:T(8,128)S(1)}, f32[512,128]{1,0:T(8,128)S(1)}) custom-call(f32[3,80,32,128]{3,2,1,0:T(8,128)} %refs_0_.1, s32[2,24]{1,0:T(2,128)} %refs_1_.3, s32[2,24]{1,0:T(2,128)} %refs_2_.3, f32[1,32,128]{2,1,0:T(8,128)} %cc_hbm.1, f32[1,32,128]{2,1,0:T(8,128)} %cr_hbm.1, f32[2,24]{1,0:T(2,128)} %refs_5_.3, ...), custom_call_target="tpu_custom_call" | custom-call | bytes 6000000 | tf_op jit(solution)/shard_map/edges_kernel/pallas_call | solution.py:517
  5.4 5.3 %collective-permute-start.1 = (f32[512,128]{1,0:T(8,128)S(1)}, f32[512,128]{1,0:T(8,128)S(1)}, u32[]{:S(2)}, u32[]{:S(2)}) collective-permute-start(f32[512,128]{1,0:T(8,128)S(1)} %get-tuple-element.18), channel_id=1, source_target_pairs={{16,32},{32,16},{48,64},{64,48},{80,96},{96,80},{112,128},{128,112... | collective-permute-start | bytes 786440 | tf_op jit(solution)/shard_map/ppermute | solution.py:533
  10.7 0.1 collective-permute-start
  10.8 3.2 %later_kernel.1.later = f32[112,128]{1,0:T(8,128)S(1)} custom-call(f32[3,32,80,128]{3,2,1,0:T(8,128)S(1)} %get-tuple-element.19.refs_0_.xt, s32[2,24]{1,0:T(2,128)} %refs_1_.3, s32[2,24]{1,0:T(2,128)} %refs_2_.3, f32[1,32,128]{2,1,0:T(8,128)} %cc_hbm.1, f32[1,32,128]{2,1,0:T(8,128)} %cr_hbm.1, f32[2,24]{1,0:T(2,128)} %refs_5_.3, f32[2,24]{1,0:T(2,128)} %refs_6_.3, ...), custom_call_target="tpu_custom_call" | custom-call | bytes 3000000 | tf_op jit(solution)/shard_map/later_kernel/pallas_call | solution.py:517
  14.0 0.8 %collective-permute-done.1.got_b = f32[512,128]{1,0:T(8,128)S(1)} collective-permute-done((f32[512,128]{1,0:T(8,128)S(1)}, f32[512,128]{1,0:T(8,128)S(1)}, u32[]{:S(2)}, u32[]{:S(2)}) %collective-permute-start.1) | collective-permute-done | bytes 262176 | tf_op jit(solution)/shard_map/ppermute | solution.py:533
  14.8 0.0 collective-permute-done.got_a
  14.8 0.5 rows_kernel.1
  15.3 3.2 %collective-permute-start.3 = (f32[352,128]{1,0:T(8,128)S(1)}, f32[352,128]{1,0:T(8,128)S(1)}, u32[]{:S(2)}, u32[]{:S(2)}) collective-permute-start(f32[352,128]{1,0:T(8,128)S(1)} %get-tuple-element.21), channel_id=1, source_target_pairs={{1,2},{2,1},{3,4},{4,3},{5,6},{6,5},{7,8},{8,7},{9,10},{10,9},{11,... | collective-permute-start | bytes 540680 | tf_op jit(solution)/shard_map/ppermute | solution.py:533
  18.5 2.0 %collective-permute-start.2 = (f32[352,128]{1,0:T(8,128)S(1)}, f32[352,128]{1,0:T(8,128)S(1)}, u32[]{:S(2)}, u32[]{:S(2)}) collective-permute-start(f32[352,128]{1,0:T(8,128)S(1)} %get-tuple-element.20.own_in), channel_id=1, source_target_pairs={{0,1},{1,0},{2,3},{3,2},{4,5},{5,4},{6,7},{7,6},{8,9},{9,8},{10,11... | collective-permute-start | bytes 540680 | tf_op jit(solution)/shard_map/ppermute | solution.py:533
  20.5 3.9 %advect_kernel.1 = (f32[3,32,80,128]{3,2,1,0:T(8,128)S(1)}, f32[32,128]{1,0:T(8,128)S(1)}) custom-call(f32[3,32,80,128]{3,2,1,0:T(8,128)S(1)} %get-tuple-element.19.refs_0_.xt, f32[512,128]{1,0:T(8,128)S(1)} %collective-permute-done.got_a, f32[512,128]{1,0:T(8,128)S(1)} %collective-permute-done.1.got_b, f32[1,32,128]{2,1,0:T(8,128)} %cc_hbm.1, ...), custom_call_target="tpu_custom_call" | custom-call | bytes 6000000 | tf_op jit(solution)/shard_map/advect_kernel/pallas_call | solution.py:517
  24.4 0.0 collective-permute-done.3.got_y
  24.4 1.0 %collective-permute-done.2.got_x = f32[352,128]{1,0:T(8,128)S(1)} collective-permute-done((f32[352,128]{1,0:T(8,128)S(1)}, f32[352,128]{1,0:T(8,128)S(1)}, u32[]{:S(2)}, u32[]{:S(2)}) %collective-permute-start.2) | collective-permute-done | bytes 180256 | tf_op jit(solution)/shard_map/ppermute | solution.py:533
  25.4 1.5 %tables_kernel.1 = (f32[112,128]{1,0:T(8,128)S(1)}, s32[1]{0:T(128)}, bf16[3,80,256]{2,1,0:T(8,128)(2,1)S(1)}, bf16[3,80,256]{2,1,0:T(8,128)(2,1)S(1)}, f32[3,3,80,128]{3,2,1,0:T(8,128)S(1)}) custom-call(f32[512,128]{1,0:T(8,128)S(1)} %get-tuple-element.17.pay, f32[512,128]{1,0:T(8,128)S(1)} %collective-permute-done.got_a, ...), custom_call_target="tpu_custom_call" | custom-call | bytes 6000000 | tf_op jit(solution)/shard_map/tables_kernel/pallas_call | solution.py:517
  26.9 4.4 %collective-permute-start.5 = (f32[112,128]{1,0:T(8,128)S(1)}, f32[112,128]{1,0:T(8,128)S(1)}, u32[]{:S(2)}, u32[]{:S(2)}) collective-permute-start(f32[112,128]{1,0:T(8,128)S(1)} %get-tuple-element.23.own), channel_id=1, source_target_pairs={{16,32},{32,16},{48,64},{64,48},{80,96},{96,80},{112,128},{128,112... | collective-permute-start | bytes 172040 | tf_op jit(solution)/shard_map/ppermute | solution.py:533
  31.4 0.1 collective-permute-start.4
  31.5 2.2 %collective-permute-done.5.b = f32[112,128]{1,0:T(8,128)S(1)} collective-permute-done((f32[112,128]{1,0:T(8,128)S(1)}, f32[112,128]{1,0:T(8,128)S(1)}, u32[]{:S(2)}, u32[]{:S(2)}) %collective-permute-start.5) | collective-permute-done | bytes 57376 | tf_op jit(solution)/shard_map/ppermute | solution.py:533
  33.6 0.0 collective-permute-done.4.a
  33.6 0.1 combine_kernel.1.own
  33.7 1.9 %collective-permute-start.7 = (f32[112,128]{1,0:T(8,128)S(1)}, f32[112,128]{1,0:T(8,128)S(1)}, u32[]{:S(2)}, u32[]{:S(2)}) collective-permute-start(f32[112,128]{1,0:T(8,128)S(1)} %combine_kernel.1.own), channel_id=1, source_target_pairs={{1,2},{2,1},{3,4},{4,3},{5,6},{6,5},{7,8},{8,7},{9,10},{10,9},{11,... | collective-permute-start | bytes 172040 | tf_op jit(solution)/shard_map/ppermute | solution.py:533
  35.7 3.5 %collective-permute-start.6 = (f32[112,128]{1,0:T(8,128)S(1)}, f32[112,128]{1,0:T(8,128)S(1)}, u32[]{:S(2)}, u32[]{:S(2)}) collective-permute-start(f32[112,128]{1,0:T(8,128)S(1)} %combine_kernel.1.own), channel_id=1, source_target_pairs={{0,1},{1,0},{2,3},{3,2},{4,5},{5,4},{6,7},{7,6},{8,9},{9,8},{10,11... | collective-permute-start | bytes 172040 | tf_op jit(solution)/shard_map/ppermute | solution.py:533
  39.2 8.4 %first_kernel.1.state = f32[3,32,80,128]{3,2,1,0:T(8,128)S(1)} custom-call(s32[1]{0:T(128)} %get-tuple-element.24.count, f32[3,32,80,128]{3,2,1,0:T(8,128)S(1)} %get-tuple-element.25.state, f32[32,128]{1,0:T(8,128)S(1)} %get-tuple-element.22.after.edge, f32[352,128]{1,0:T(8,128)S(1)} %collective-permute-done.2.got_x, ...), custom_call_target="tpu_custom_call" | custom-call | bytes 12000000 | tf_op jit(solution)/shard_map/first_kernel/pallas_call | solution.py:517
  47.6 0.0 collective-permute-done.7.got_y
  47.6 0.0 collective-permute-done.6.got_x
  47.7 8.0 %second_kernel.1 = f32[3,80,32,128]{3,2,1,0:T(8,128)} custom-call(f32[112,128]{1,0:T(8,128)S(1)} %combine_kernel.1.own, f32[112,128]{1,0:T(8,128)S(1)} %collective-permute-done.6.got_x, f32[112,128]{1,0:T(8,128)S(1)} %collective-permute-done.7.got_y, f32[3,32,80,128]{3,2,1,0:T(8,128)S(1)} %first_kernel.1.state), custom_call_target="tpu_custom_call" | custom-call | bytes 18000000 | tf_op jit(solution)/shard_map/second_kernel/pallas_call | solution.py:517
Async XLA Ops:
  5.4 9.4 %collective-permute-start.1 = (f32[512,128]{1,0:T(8,128)S(1)}, f32[512,128]{1,0:T(8,128)S(1)}, u32[]{:S(2)}, u32[]{:S(2)}) collective-permute-start(f32[512,128]{1,0:T(8,128)S(1)} %get-tuple-element.18), channel_id=1, source_target_pairs={{16,32},{32,16},{48,64},{64,48},{80,96},{96,80},{112,128},{128,112... | collective-permute-start | bytes 786440 | tf_op jit(solution)/shard_map/ppermute | solution.py:533
  10.7 4.0 %collective-permute-start = (f32[512,128]{1,0:T(8,128)S(1)}, f32[512,128]{1,0:T(8,128)S(1)}, u32[]{:S(2)}, u32[]{:S(2)}) collective-permute-start(f32[512,128]{1,0:T(8,128)S(1)} %get-tuple-element.17.pay), channel_id=1, source_target_pairs={{0,16},{16,0},{32,48},{48,32},{64,80},{80,64},{96,112},{112,96},{1... | collective-permute-start | bytes 786440 | tf_op jit(solution)/shard_map/ppermute | solution.py:533
  15.3 9.1 %collective-permute-start.3 = (f32[352,128]{1,0:T(8,128)S(1)}, f32[352,128]{1,0:T(8,128)S(1)}, u32[]{:S(2)}, u32[]{:S(2)}) collective-permute-start(f32[352,128]{1,0:T(8,128)S(1)} %get-tuple-element.21), channel_id=1, source_target_pairs={{1,2},{2,1},{3,4},{4,3},{5,6},{6,5},{7,8},{8,7},{9,10},{10,9},{11,... | collective-permute-start | bytes 540680 | tf_op jit(solution)/shard_map/ppermute | solution.py:533
  18.5 6.9 %collective-permute-start.2 = (f32[352,128]{1,0:T(8,128)S(1)}, f32[352,128]{1,0:T(8,128)S(1)}, u32[]{:S(2)}, u32[]{:S(2)}) collective-permute-start(f32[352,128]{1,0:T(8,128)S(1)} %get-tuple-element.20.own_in), channel_id=1, source_target_pairs={{0,1},{1,0},{2,3},{3,2},{4,5},{5,4},{6,7},{7,6},{8,9},{9,8},{10,11... | collective-permute-start | bytes 540680 | tf_op jit(solution)/shard_map/ppermute | solution.py:533
  26.9 6.7 %collective-permute-start.5 = (f32[112,128]{1,0:T(8,128)S(1)}, f32[112,128]{1,0:T(8,128)S(1)}, u32[]{:S(2)}, u32[]{:S(2)}) collective-permute-start(f32[112,128]{1,0:T(8,128)S(1)} %get-tuple-element.23.own), channel_id=1, source_target_pairs={{16,32},{32,16},{48,64},{64,48},{80,96},{96,80},{112,128},{128,112... | collective-permute-start | bytes 172040 | tf_op jit(solution)/shard_map/ppermute | solution.py:533
  31.4 2.3 %collective-permute-start.4 = (f32[112,128]{1,0:T(8,128)S(1)}, f32[112,128]{1,0:T(8,128)S(1)}, u32[]{:S(2)}, u32[]{:S(2)}) collective-permute-start(f32[112,128]{1,0:T(8,128)S(1)} %get-tuple-element.23.own), channel_id=1, source_target_pairs={{0,16},{16,0},{32,48},{48,32},{64,80},{80,64},{96,112},{112,96},{1... | collective-permute-start | bytes 172040 | tf_op jit(solution)/shard_map/ppermute | solution.py:533
  33.7 13.9 %collective-permute-start.7 = (f32[112,128]{1,0:T(8,128)S(1)}, f32[112,128]{1,0:T(8,128)S(1)}, u32[]{:S(2)}, u32[]{:S(2)}) collective-permute-start(f32[112,128]{1,0:T(8,128)S(1)} %combine_kernel.1.own), channel_id=1, source_target_pairs={{1,2},{2,1},{3,4},{4,3},{5,6},{6,5},{7,8},{8,7},{9,10},{10,9},{11,... | collective-permute-start | bytes 172040 | tf_op jit(solution)/shard_map/ppermute | solution.py:533
  35.7 12.0 %collective-permute-start.6 = (f32[112,128]{1,0:T(8,128)S(1)}, f32[112,128]{1,0:T(8,128)S(1)}, u32[]{:S(2)}, u32[]{:S(2)}) collective-permute-start(f32[112,128]{1,0:T(8,128)S(1)} %combine_kernel.1.own), channel_id=1, source_target_pairs={{0,1},{1,0},{2,3},{3,2},{4,5},{5,4},{6,7},{7,6},{8,9},{9,8},{10,11... | collective-permute-start | bytes 172040 | tf_op jit(solution)/shard_map/ppermute | solution.py:533

commit v2 on v1

--- a/solution.py
+++ b/solution.py
@@ -11,6 +11,7 @@
 VALUE, ERROR, LIVE = GAIN, INNOV, ALPHA
 LATER = 96
 S = 80
+STEP = 4
 f32, bf16 = jnp.float32, jnp.bfloat16
 VMEM = pltpu.VMEM
 MiB = 1 << 20
@@ -54,33 +55,41 @@
 
 
 def own_part(b, start, xt, cell, kind, cc, cr, value, error, live, listed, part):
-    lane, lane1 = lanes((M, C)), lanes((1, C))
+    lane, lane1, lane8 = lanes((M, C)), lanes((1, C)), lanes((8, C))
+    sub8 = subs((8, C))
     zero = jnp.zeros((1, C), f32)
     prior = jnp.zeros((M, C), f32)
-    rows = [zero] * 7
+    coefs = jnp.zeros((8, C), f32)
+    rows = [zero] * 3
     for s in range(K):
         at = cell[b, s]
-        r, c = at // C, at % C
+        r, c = lax.shift_right_logical(at, 7), lax.bitwise_and(at, C - 1)
         f = kind[b, s]
         rf = zero + r.astype(f32)
-        here, ae, aw, an, as_ = stencil(cc[0, pl.ds(r, 1), :], cr[0, pl.ds(r, 1), :])
-        turn = lax.rem(start + s + C - c, C)
-        fields = [rf, zero + c.astype(f32), zero + f.astype(f32)]
-        fields += [pltpu.roll(w, turn, 1) for w in (ae, aw, an, as_)]
         mine1 = lane1 == start + s
+        fields = (rf, zero + c.astype(f32), zero + f.astype(f32))
         rows = [jnp.where(mine1, w, old) for w, old in zip(fields, rows)]
-        ae = jnp.where(lane1 == C - 1, 0.0, ae)
-        aw = jnp.where(lane1 == 0, 0.0, aw)
+        here, ae, aw, an, as_ = (
+            jnp.where(lane1 == c, w, 0.0)
+            for w in stencil(cc[0, pl.ds(r, 1), :], cr[0, pl.ds(r, 1), :])
+        )
+        stack = jnp.where(
+            sub8 == 0, ae, jnp.where(sub8 == 1, aw, jnp.where(sub8 == 2, an, as_))
+        )
+        total = jnp.sum(stack, axis=1, keepdims=True)
+        coefs = jnp.where(lane8 == start + s, total, coefs)
+        ae = pltpu.roll(jnp.where(lane1 == C - 1, 0.0, ae), 1, 1)
+        aw = pltpu.roll(jnp.where(lane1 == 0, 0.0, aw), C - 1, 1)
         an = jnp.where(rf == R - 1.0, 0.0, an)
         as_ = jnp.where(rf == 0.0, 0.0, as_)
-        x = xt[f, r]
-        y = here * x + ae * pltpu.roll(x, C - 1, 1) + aw * pltpu.roll(x, 1, 1)
+        y = (here + ae + aw) * xt[f, r]
         y = y + an * xt[f, jnp.minimum(r + 1, R - 1)] + as_ * xt[f, jnp.maximum(r - 1, 0)]
-        prior = jnp.where(lane == start + s, pltpu.roll(y, turn, 1), prior)
+        prior = jnp.where(lane == start + s, jnp.sum(y, axis=1, keepdims=True), prior)
     part[...] = jnp.zeros((T, C), f32)
     part[:M] = prior
-    for n, w in zip((ROW, COL, KIND, AE, AW, AN, AS), rows):
+    for n, w in zip((ROW, COL, KIND), rows):
         part[n : n + 1, :] = w
+    part[AE : AE + 8, :] = coefs
     keep = slice(start, start + K)
     part[VALUE : VALUE + 1, keep] = value[b : b + 1, :]
     part[ERROR : ERROR + 1, keep] = error[b : b + 1, :]
@@ -418,15 +427,16 @@
         def local(i):
             return taper(locs[j, 0] - i.astype(f32)) * col_w[...]
 
-        def body(n, carry):
-            i = 2 * n
-            lw = jnp.concatenate([local(i), local(i + 1)], axis=1)
-            for f in range(F):
-                pair = row_of(f, i, 0), row_of(f, i + 1, 1)
-                d = update(jnp.concatenate(pair, axis=1), lw, ycat[j], bcat[j])
-                if base is not None:
-                    pair = base[f, i], base[f, i + 1]
-                put(n, f, pair[0] + d[:, :C], pair[1] + d[:, C:])
+        def body(step, carry):
+            for n in [step * STEP + u for u in range(STEP)]:
+                i = 2 * n
+                lw = jnp.concatenate([local(i), local(i + 1)], axis=1)
+                for f in range(F):
+                    pair = row_of(f, i, 0), row_of(f, i + 1, 1)
+                    d = update(jnp.concatenate(pair, axis=1), lw, ycat[j], bcat[j])
+                    if base is not None:
+                        pair = base[f, i], base[f, i + 1]
+                    put(n, f, pair[0] + d[:, :C], pair[1] + d[:, C:])
             return carry
 
         return body
@@ -438,12 +448,12 @@
     @pl.when(count > S)
     def _():
         weigh(1)
-        lax.fori_loop(0, R // 2, sweep(None, 1, keep), 0)
+        lax.fori_loop(0, R // 2 // STEP, sweep(None, 1, keep), 0)
 
         @pl.when(count > 2 * S)
         def _():
             weigh(2)
-            lax.fori_loop(0, R // 2, sweep(total, 2, keep), 0)
+            lax.fori_loop(0, R // 2 // STEP, sweep(total, 2, keep), 0)
 
         weigh(0)
         emit(sweep, total)
@@ -466,7 +476,7 @@
             out[f, 2 * n] = a
             out[f, 2 * n + 1] = b
 
-        lax.fori_loop(0, R // 2, sweep(base, 0, put), 0)
+        lax.fori_loop(0, R // 2 // STEP, sweep(base, 0, put), 0)
 
     sweeps(row_of, count[0], ycat, bcat, locs, col_w, total, emit)
 
@@ -495,7 +505,7 @@
                 rows[pl.ds(r, M, stride=8), :] = a
                 rows[pl.ds(r + 1, M, stride=8), :] = b
 
-            lax.fori_loop(4 * ib, 4 * ib + 4, sweep(base, 0, put), 0)
+            lax.fori_loop(4 * ib // STEP, (4 * ib + 4) // STEP, sweep(base, 0, put), 0)
             for f in range(F):
                 copy(ib, f).start()
 

time: 56.2 us -> 48.4 us (0.86)
  Pallas kernels: 31 us -> 22.8 us
    pallas_call x8, Pallas kernels: 31 us -> 22.8 us  [call(): pl.pallas_call(kernel, out_shape=outs, in_specs=[pl.BlockSpec(memory_spac...]
  transfers between devices with their start and end apart: 8 -> 8, of which waited for: 3 -> 3; matrix products, arithmetic and copies ran while one was open for 0% -> 0% of each run, Pallas kernels for 28% -> 23%
where the time goes in v2:
time: 48.4 us; the launch traced here: 47.9 us
  Pallas kernels  22.8 us (47%)
  starting transfers between devices  20.5 us (42%)
  waiting for transfers between devices  4.34 us (9%)
    pallas_call x8, Pallas kernels, call(): pl.pallas_call(kernel, out_shape=outs, in_specs=[pl.BlockSpec(memory_spac...  22.8 us
    ppermute x8, starting transfers between devices, swap(): return lax.ppermute(x, axis, pairs)  20.5 us
    ppermute x8, waiting for transfers between devices, swap(): return lax.ppermute(x, axis, pairs)  4.34 us
  transfers between devices with their start and end apart: 8, of which 3 were waited for; matrix products, arithmetic and copies ran while one was open for 0% of the time, Pallas kernels for 23%

profile of v2, /device:TPU:111, one launch (start us, length us, event | category | flops | bytes accessed | tf_op | source)
XLA Modules:
  0.0 47.9 jit_solution(17475015133845832549)
XLA Ops:
  0.0 5.1 %edges_kernel.1 = (f32[3,32,80,128]{3,2,1,0:T(8,128)S(1)}, f32[512,128]{1,0:T(8,128)S(1)}, f32[512,128]{1,0:T(8,128)S(1)}) custom-call(f32[3,80,32,128]{3,2,1,0:T(8,128)} %refs_0_.1, s32[2,24]{1,0:T(2,128)} %refs_1_.3, s32[2,24]{1,0:T(2,128)} %refs_2_.3, f32[1,32,128]{2,1,0:T(8,128)} %cc_hbm.1, f32[1,32,128]{2,1,0:T(8,128)} %cr_hbm.1, f32[2,24]{1,0:T(2,128)} %refs_5_.3, ...), custom_call_target="tpu_custom_call" | custom-call | bytes 6000000 | tf_op jit(solution)/shard_map/edges_kernel/pallas_call | solution.py:527
  5.1 5.3 %collective-permute-start.1 = (f32[512,128]{1,0:T(8,128)S(1)}, f32[512,128]{1,0:T(8,128)S(1)}, u32[]{:S(2)}, u32[]{:S(2)}) collective-permute-start(f32[512,128]{1,0:T(8,128)S(1)} %get-tuple-element.18), channel_id=1, source_target_pairs={{16,32},{32,16},{48,64},{64,48},{80,96},{96,80},{112,128},{128,112... | collective-permute-start | bytes 786440 | tf_op jit(solution)/shard_map/ppermute | solution.py:543
  10.5 0.1 collective-permute-start
  10.6 2.9 %later_kernel.1.later = f32[112,128]{1,0:T(8,128)S(1)} custom-call(f32[3,32,80,128]{3,2,1,0:T(8,128)S(1)} %get-tuple-element.19.refs_0_.xt, s32[2,24]{1,0:T(2,128)} %refs_1_.3, s32[2,24]{1,0:T(2,128)} %refs_2_.3, f32[1,32,128]{2,1,0:T(8,128)} %cc_hbm.1, f32[1,32,128]{2,1,0:T(8,128)} %cr_hbm.1, f32[2,24]{1,0:T(2,128)} %refs_5_.3, f32[2,24]{1,0:T(2,128)} %refs_6_.3, ...), custom_call_target="tpu_custom_call" | custom-call | bytes 3000000 | tf_op jit(solution)/shard_map/later_kernel/pallas_call | solution.py:527
  13.5 1.0 %collective-permute-done.1.got_b = f32[512,128]{1,0:T(8,128)S(1)} collective-permute-done((f32[512,128]{1,0:T(8,128)S(1)}, f32[512,128]{1,0:T(8,128)S(1)}, u32[]{:S(2)}, u32[]{:S(2)}) %collective-permute-start.1) | collective-permute-done | bytes 262176 | tf_op jit(solution)/shard_map/ppermute | solution.py:543
  14.5 0.0 collective-permute-done.got_a
  14.5 0.5 %rows_kernel.1 = (f32[352,128]{1,0:T(8,128)S(1)}, f32[352,128]{1,0:T(8,128)S(1)}) custom-call(f32[3,32,80,128]{3,2,1,0:T(8,128)S(1)} %get-tuple-element.19.refs_0_.xt, f32[512,128]{1,0:T(8,128)S(1)} %get-tuple-element.17.pay, f32[112,128]{1,0:T(8,128)S(1)} %later_kernel.1.later, f32[512,128]{1,0:T(8,128)S(1)} %collective-permute-done.got_a, ...), custom_call_target="tpu_custom_call" | custom-call | bytes 6000000 | tf_op jit(solution)/shard_map/rows_kernel/pallas_call | solution.py:527
  15.0 3.2 %collective-permute-start.3 = (f32[352,128]{1,0:T(8,128)S(1)}, f32[352,128]{1,0:T(8,128)S(1)}, u32[]{:S(2)}, u32[]{:S(2)}) collective-permute-start(f32[352,128]{1,0:T(8,128)S(1)} %get-tuple-element.21), channel_id=1, source_target_pairs={{1,2},{2,1},{3,4},{4,3},{5,6},{6,5},{7,8},{8,7},{9,10},{10,9},{11,... | collective-permute-start | bytes 540680 | tf_op jit(solution)/shard_map/ppermute | solution.py:543
  18.2 2.0 %collective-permute-start.2 = (f32[352,128]{1,0:T(8,128)S(1)}, f32[352,128]{1,0:T(8,128)S(1)}, u32[]{:S(2)}, u32[]{:S(2)}) collective-permute-start(f32[352,128]{1,0:T(8,128)S(1)} %get-tuple-element.20.own_in), channel_id=1, source_target_pairs={{0,1},{1,0},{2,3},{3,2},{4,5},{5,4},{6,7},{7,6},{8,9},{9,8},{10,11... | collective-permute-start | bytes 540680 | tf_op jit(solution)/shard_map/ppermute | solution.py:543
  20.2 3.9 %advect_kernel.1 = (f32[3,32,80,128]{3,2,1,0:T(8,128)S(1)}, f32[32,128]{1,0:T(8,128)S(1)}) custom-call(f32[3,32,80,128]{3,2,1,0:T(8,128)S(1)} %get-tuple-element.19.refs_0_.xt, f32[512,128]{1,0:T(8,128)S(1)} %collective-permute-done.got_a, f32[512,128]{1,0:T(8,128)S(1)} %collective-permute-done.1.got_b, f32[1,32,128]{2,1,0:T(8,128)} %cc_hbm.1, ...), custom_call_target="tpu_custom_call" | custom-call | bytes 6000000 | tf_op jit(solution)/shard_map/advect_kernel/pallas_call | solution.py:527
  24.1 0.0 collective-permute-done.3.got_y
  24.1 1.1 %collective-permute-done.2.got_x = f32[352,128]{1,0:T(8,128)S(1)} collective-permute-done((f32[352,128]{1,0:T(8,128)S(1)}, f32[352,128]{1,0:T(8,128)S(1)}, u32[]{:S(2)}, u32[]{:S(2)}) %collective-permute-start.2) | collective-permute-done | bytes 180256 | tf_op jit(solution)/shard_map/ppermute | solution.py:543
  25.2 1.5 %tables_kernel.1 = (f32[112,128]{1,0:T(8,128)S(1)}, s32[1]{0:T(128)}, bf16[3,80,256]{2,1,0:T(8,128)(2,1)S(1)}, bf16[3,80,256]{2,1,0:T(8,128)(2,1)S(1)}, f32[3,3,80,128]{3,2,1,0:T(8,128)S(1)}) custom-call(f32[512,128]{1,0:T(8,128)S(1)} %get-tuple-element.17.pay, f32[512,128]{1,0:T(8,128)S(1)} %collective-permute-done.got_a, ...), custom_call_target="tpu_custom_call" | custom-call | bytes 6000000 | tf_op jit(solution)/shard_map/tables_kernel/pallas_call | solution.py:527
  26.8 4.4 %collective-permute-start.5 = (f32[112,128]{1,0:T(8,128)S(1)}, f32[112,128]{1,0:T(8,128)S(1)}, u32[]{:S(2)}, u32[]{:S(2)}) collective-permute-start(f32[112,128]{1,0:T(8,128)S(1)} %get-tuple-element.23.own), channel_id=1, source_target_pairs={{16,32},{32,16},{48,64},{64,48},{80,96},{96,80},{112,128},{128,112... | collective-permute-start | bytes 172040 | tf_op jit(solution)/shard_map/ppermute | solution.py:543
  31.1 0.1 collective-permute-start.4
  31.2 2.2 %collective-permute-done.5.b = f32[112,128]{1,0:T(8,128)S(1)} collective-permute-done((f32[112,128]{1,0:T(8,128)S(1)}, f32[112,128]{1,0:T(8,128)S(1)}, u32[]{:S(2)}, u32[]{:S(2)}) %collective-permute-start.5) | collective-permute-done | bytes 57376 | tf_op jit(solution)/shard_map/ppermute | solution.py:543
  33.5 0.0 collective-permute-done.4.a
  33.5 0.1 combine_kernel.1.own
  33.6 1.9 %collective-permute-start.7 = (f32[112,128]{1,0:T(8,128)S(1)}, f32[112,128]{1,0:T(8,128)S(1)}, u32[]{:S(2)}, u32[]{:S(2)}) collective-permute-start(f32[112,128]{1,0:T(8,128)S(1)} %combine_kernel.1.own), channel_id=1, source_target_pairs={{1,2},{2,1},{3,4},{4,3},{5,6},{6,5},{7,8},{8,7},{9,10},{10,9},{11,... | collective-permute-start | bytes 172040 | tf_op jit(solution)/shard_map/ppermute | solution.py:543
  35.5 3.5 %collective-permute-start.6 = (f32[112,128]{1,0:T(8,128)S(1)}, f32[112,128]{1,0:T(8,128)S(1)}, u32[]{:S(2)}, u32[]{:S(2)}) collective-permute-start(f32[112,128]{1,0:T(8,128)S(1)} %combine_kernel.1.own), channel_id=1, source_target_pairs={{0,1},{1,0},{2,3},{3,2},{4,5},{5,4},{6,7},{7,6},{8,9},{9,8},{10,11... | collective-permute-start | bytes 172040 | tf_op jit(solution)/shard_map/ppermute | solution.py:543
  39.0 4.2 %first_kernel.1.state = f32[3,32,80,128]{3,2,1,0:T(8,128)S(1)} custom-call(s32[1]{0:T(128)} %get-tuple-element.24.count, f32[3,32,80,128]{3,2,1,0:T(8,128)S(1)} %get-tuple-element.25.state, f32[32,128]{1,0:T(8,128)S(1)} %get-tuple-element.22.after.edge, f32[352,128]{1,0:T(8,128)S(1)} %collective-permute-done.2.got_x, ...), custom_call_target="tpu_custom_call" | custom-call | bytes 12000000 | tf_op jit(solution)/shard_map/first_kernel/pallas_call | solution.py:527
  43.3 0.0 collective-permute-done.7.got_y
  43.3 0.0 collective-permute-done.6.got_x
  43.3 4.5 %second_kernel.1 = f32[3,80,32,128]{3,2,1,0:T(8,128)} custom-call(f32[112,128]{1,0:T(8,128)S(1)} %combine_kernel.1.own, f32[112,128]{1,0:T(8,128)S(1)} %collective-permute-done.6.got_x, f32[112,128]{1,0:T(8,128)S(1)} %collective-permute-done.7.got_y, f32[3,32,80,128]{3,2,1,0:T(8,128)S(1)} %first_kernel.1.state), custom_call_target="tpu_custom_call" | custom-call | bytes 18000000 | tf_op jit(solution)/shard_map/second_kernel/pallas_call | solution.py:527
Async XLA Ops:
  5.1 9.4 %collective-permute-start.1 = (f32[512,128]{1,0:T(8,128)S(1)}, f32[512,128]{1,0:T(8,128)S(1)}, u32[]{:S(2)}, u32[]{:S(2)}) collective-permute-start(f32[512,128]{1,0:T(8,128)S(1)} %get-tuple-element.18), channel_id=1, source_target_pairs={{16,32},{32,16},{48,64},{64,48},{80,96},{96,80},{112,128},{128,112... | collective-permute-start | bytes 786440 | tf_op jit(solution)/shard_map/ppermute | solution.py:543
  10.5 4.0 %collective-permute-start = (f32[512,128]{1,0:T(8,128)S(1)}, f32[512,128]{1,0:T(8,128)S(1)}, u32[]{:S(2)}, u32[]{:S(2)}) collective-permute-start(f32[512,128]{1,0:T(8,128)S(1)} %get-tuple-element.17.pay), channel_id=1, source_target_pairs={{0,16},{16,0},{32,48},{48,32},{64,80},{80,64},{96,112},{112,96},{1... | collective-permute-start | bytes 786440 | tf_op jit(solution)/shard_map/ppermute | solution.py:543
  15.0 9.1 %collective-permute-start.3 = (f32[352,128]{1,0:T(8,128)S(1)}, f32[352,128]{1,0:T(8,128)S(1)}, u32[]{:S(2)}, u32[]{:S(2)}) collective-permute-start(f32[352,128]{1,0:T(8,128)S(1)} %get-tuple-element.21), channel_id=1, source_target_pairs={{1,2},{2,1},{3,4},{4,3},{5,6},{6,5},{7,8},{8,7},{9,10},{10,9},{11,... | collective-permute-start | bytes 540680 | tf_op jit(solution)/shard_map/ppermute | solution.py:543
  18.2 7.0 %collective-permute-start.2 = (f32[352,128]{1,0:T(8,128)S(1)}, f32[352,128]{1,0:T(8,128)S(1)}, u32[]{:S(2)}, u32[]{:S(2)}) collective-permute-start(f32[352,128]{1,0:T(8,128)S(1)} %get-tuple-element.20.own_in), channel_id=1, source_target_pairs={{0,1},{1,0},{2,3},{3,2},{4,5},{5,4},{6,7},{7,6},{8,9},{9,8},{10,11... | collective-permute-start | bytes 540680 | tf_op jit(solution)/shard_map/ppermute | solution.py:543
  26.8 6.7 %collective-permute-start.5 = (f32[112,128]{1,0:T(8,128)S(1)}, f32[112,128]{1,0:T(8,128)S(1)}, u32[]{:S(2)}, u32[]{:S(2)}) collective-permute-start(f32[112,128]{1,0:T(8,128)S(1)} %get-tuple-element.23.own), channel_id=1, source_target_pairs={{16,32},{32,16},{48,64},{64,48},{80,96},{96,80},{112,128},{128,112... | collective-permute-start | bytes 172040 | tf_op jit(solution)/shard_map/ppermute | solution.py:543
  31.1 2.3 %collective-permute-start.4 = (f32[112,128]{1,0:T(8,128)S(1)}, f32[112,128]{1,0:T(8,128)S(1)}, u32[]{:S(2)}, u32[]{:S(2)}) collective-permute-start(f32[112,128]{1,0:T(8,128)S(1)} %get-tuple-element.23.own), channel_id=1, source_target_pairs={{0,16},{16,0},{32,48},{48,32},{64,80},{80,64},{96,112},{112,96},{1... | collective-permute-start | bytes 172040 | tf_op jit(solution)/shard_map/ppermute | solution.py:543
  33.6 9.7 %collective-permute-start.7 = (f32[112,128]{1,0:T(8,128)S(1)}, f32[112,128]{1,0:T(8,128)S(1)}, u32[]{:S(2)}, u32[]{:S(2)}) collective-permute-start(f32[112,128]{1,0:T(8,128)S(1)} %combine_kernel.1.own), channel_id=1, source_target_pairs={{1,2},{2,1},{3,4},{4,3},{5,6},{6,5},{7,8},{8,7},{9,10},{10,9},{11,... | collective-permute-start | bytes 172040 | tf_op jit(solution)/shard_map/ppermute | solution.py:543
  35.5 7.8 %collective-permute-start.6 = (f32[112,128]{1,0:T(8,128)S(1)}, f32[112,128]{1,0:T(8,128)S(1)}, u32[]{:S(2)}, u32[]{:S(2)}) collective-permute-start(f32[112,128]{1,0:T(8,128)S(1)} %combine_kernel.1.own), channel_id=1, source_target_pairs={{0,1},{1,0},{2,3},{3,2},{4,5},{5,4},{6,7},{7,6},{8,9},{9,8},{10,11... | collective-permute-start | bytes 172040 | tf_op jit(solution)/shard_map/ppermute | solution.py:543

commit v3 on v2

--- a/solution.py
+++ b/solution.py
@@ -9,6 +9,7 @@
 GAIN, INNOV, ALPHA, ROW, COL, KIND = 80, 81, 82, 83, 84, 85
 AE, AW, AN, AS, LIST, T = 88, 89, 90, 91, 96, 112
 VALUE, ERROR, LIVE = GAIN, INNOV, ALPHA
+SPARE = 96
 LATER = 96
 S = 80
 STEP = 4
@@ -24,13 +25,6 @@
 def split(x):
     hi = x.astype(bf16)
     return hi, (x - hi.astype(f32)).astype(bf16)
-
-
-def split3(x):
-    hi = x.astype(bf16)
-    rest = x - hi.astype(f32)
-    mid = rest.astype(bf16)
-    return hi, mid, (rest - mid.astype(f32)).astype(bf16)
 
 
 def dot(a, b, dims=((1,), (0,))):
@@ -140,15 +134,15 @@
     for f in range(F):
         pay_a[pl.ds(f * M, M), :] = xt[f, ra]
         pay_b[pl.ds(f * M, M), :] = xt[f, rb]
+    for c in copies:
+        c.wait()
+    part = acc.at[2]
+    own_part(0, SPARE, xt, *here, part)
+    first = first + part[:M]
     for pay in (pay_a, pay_b):
         pay[pl.ds(F * M, M), :] = first
         pay[pl.ds(F * M + M, M), :] = last
-    for c in copies:
-        c.wait()
-    part = acc.at[2]
-    own_part(0, 0, xt, *here, part)
-    pay_a[pl.ds(5 * M, T), :] = part[...]
-    pay_b[pl.ds(5 * M, T), :] = part[...]
+        pay[pl.ds(5 * M, T - M), :] = part[M:]
 
 
 def later_kernel(*refs):
@@ -178,14 +172,20 @@
 
 def pickup(sources, key):
     hot = (subs((F * C, C)).astype(f32) == key).astype(f32).astype(bf16)
-    return sum(dot(h, hot) for h in split3(jnp.concatenate(sources, axis=1)))
-
-
-def rows_kernel(xt, pay, later, got_a, got_b, out_a, out_b):
+    return sum(dot(h, hot) for h in split(jnp.concatenate(sources, axis=1)))
+
+
+def spare_only(x):
+    lane = lanes(x.shape)
+    return jnp.where((lane >= SPARE) & (lane < SPARE + K), x, 0.0)
+
+
+def rows_kernel(xt, pay, later, got_a, got_b, out_a, out_b, own):
     pa, pb = parity("lat"), parity("lon")
-    base = 5 * M
-    comb = combine(pay[pl.ds(base, T), :], got_a[pl.ds(base, T), :], got_b[pl.ds(base, T), :])
-    comb = comb + later[...]
+    comb = later[...]
+    for n, src in enumerate((pay, got_a, got_b)):
+        part = jnp.concatenate([src[pl.ds(F * M, M), :], src[pl.ds(5 * M, T - M), :]], axis=0)
+        comb = comb + pltpu.roll(spare_only(part), C - SPARE + n * K, 1)
     row, col, kind = comb[ROW : ROW + 1], comb[COL : COL + 1], comb[KIND : KIND + 1]
     group = lane_group()
     edge_a = jnp.where(pa == 1, 0, R - 1)
@@ -204,11 +204,14 @@
     odd = flag(pb, (M, C))
     for n, src in enumerate((pay, got_a, got_b)):
         first, last = src[pl.ds(F * M, M), :], src[pl.ds(F * M + M, M), :]
-        out_a[pl.ds(n * M, M), :] = jnp.where(odd, first, last)
-        out_b[pl.ds(n * M, M), :] = jnp.where(odd, last, first)
+        column = lanes((M, C)) < SPARE
+        mine = spare_only(pltpu.roll(prior, SPARE - n * K, 1))
+        out_a[pl.ds(n * M, M), :] = jnp.where(column, jnp.where(odd, first, last), mine)
+        out_b[pl.ds(n * M, M), :] = jnp.where(column, jnp.where(odd, last, first), mine)
     for out in (out_a, out_b):
-        out[pl.ds(3 * M, M), :] = prior
-        out[pl.ds(4 * M, T - M), :] = comb[M:]
+        out[pl.ds(3 * M, T - M), :] = comb[M:]
+    own[:M] = prior
+    own[M:] = comb[M:]
 
 
 def statistics(t):
@@ -274,7 +277,7 @@
     p = subs((C, F * C)).astype(f32) + jnp.asarray(chunk * S, f32)
     own = subs((C, F * C)) < S
     pick = ((rank == p) & own).astype(f32).astype(bf16)
-    turned = sum(dot(t, pick, ((1,), (1,))) for t in split3(fields))
+    turned = sum(dot(t, pick, ((1,), (1,))) for t in split(fields))
     chosen = jnp.concatenate([turned, jnp.zeros((32, C), f32)], axis=0).T[:S]
     ycat[chunk] = spread_lanes(*split(chosen))
     back = turned[INNOV : INNOV + 1, :] - turned[ALPHA : ALPHA + 1, :] * turned[:M]
@@ -309,7 +312,9 @@
     return dot(bcat, jnp.concatenate([hi, hi, lo, none], axis=0))
 
 
-def tables_kernel(pay, got_a, got_b, own_in, got_x, got_y, after, table, count_out, ycat, bcat, locs):
+def tables_kernel(
+    pay, got_a, got_b, own_in, got_x, got_y, after, table, count_out, ycat, bcat, locs, sides
+):
     pb = parity("lon")
     edge_x = jnp.where(pb == 1, 0.0, C - 1.0)
     edge_y = C - 1.0 - edge_x
@@ -333,15 +338,19 @@
     def packs(got):
         return [got[pl.ds(n * M, M), :] for n in range(3)]
 
-    base = 3 * M
+    for side, got in enumerate((got_x, got_y)):
+        sides[side, :M] = sum(
+            pltpu.roll(spare_only(h), C - SPARE + n * K, 1) for n, h in enumerate(packs(got))
+        )
+        sides[side, M:] = got[pl.ds(3 * M, T - M), :]
     out = []
     later = None
     for index, (src, parts) in enumerate((
         (own_in, ((packs(got_x), edge_x), (packs(got_y), edge_y))),
-        (got_x, ((mine_x, edge_y),)),
-        (got_y, ((mine_y, edge_x),)),
+        (sides.at[0], ((mine_x, edge_y),)),
+        (sides.at[1], ((mine_y, edge_x),)),
     )):
-        raw = src.at[pl.ds(base, T), :]
+        raw = src
         t = raw[...]
         whole = jnp.concatenate([complete(t, parts), t[M:]], axis=0)
         if index == 0:
@@ -419,12 +428,15 @@
     merged[1] = jnp.where(odd_lane, west, east)
 
 
-def sweeps(row_of, count, ycat, bcat, locs, col_w, total, emit):
+def sweeps(row_of, count, ycat, bcat, locs, row_w, col_w, total, emit):
     def weigh(j):
+        row_w[...] = taper(locs[j, 0] - lanes((S, C)).astype(f32))
         col_w[...] = taper(locs[j, 1] - lanes((S, C)).astype(f32)) * locs[j, 2]
 
     def sweep(base, j, put):
         def local(i):
+            if isinstance(i, int):
+                return jnp.broadcast_to(row_w[:, i : i + 1], (S, C)) * col_w[...]
             return taper(locs[j, 0] - i.astype(f32)) * col_w[...]
 
         def body(step, carry):
@@ -464,7 +476,7 @@
         emit(sweep, None)
 
 
-def first_kernel(count, state, edge, got_x, got_y, ycat, bcat, locs, out, col_w, total, merged):
+def first_kernel(count, state, edge, got_x, got_y, ycat, bcat, locs, out, row_w, col_w, total, merged):
     lay_halos(got_x, got_y, merged)
 
     def row_of(f, i, odd):
@@ -478,10 +490,10 @@
 
         lax.fori_loop(0, R // 2 // STEP, sweep(base, 0, put), 0)
 
-    sweeps(row_of, count[0], ycat, bcat, locs, col_w, total, emit)
-
-
-def second_kernel(own, got_x, got_y, state, out, buf, sem, ycat, bcat, locs, col_w, total):
+    sweeps(row_of, count[0], ycat, bcat, locs, row_w, col_w, total, emit)
+
+
+def second_kernel(own, got_x, got_y, state, out, buf, sem, ycat, bcat, locs, row_w, col_w, total):
     parts = []
     for index, raw in enumerate((own, got_x, got_y)):
         t = raw[...]
@@ -505,11 +517,12 @@
                 rows[pl.ds(r, M, stride=8), :] = a
                 rows[pl.ds(r + 1, M, stride=8), :] = b
 
-            lax.fori_loop(4 * ib // STEP, (4 * ib + 4) // STEP, sweep(base, 0, put), 0)
+            for step in range(4 * ib // STEP, (4 * ib + 4) // STEP):
+                sweep(base, 0, put)(step, 0)
             for f in range(F):
                 copy(ib, f).start()
 
-    sweeps(lambda f, i, odd: state[f, i], count, ycat, bcat, locs, col_w, total, emit)
+    sweeps(lambda f, i, odd: state[f, i], count, ycat, bcat, locs, row_w, col_w, total, emit)
     for ib in range(R // 8):
         for f in range(F):
             copy(ib, f).wait()
@@ -558,7 +571,7 @@
     held = [(pltpu.SMEM if n < 2 else VMEM)(a.shape, a.dtype) for n, a in enumerate(small)]
     held_sems = pltpu.SemaphoreType.DMA((len(small),))
 
-    pay_shape = sds((5 * M + T, C), f32)
+    pay_shape = sds((4 * M + T, C), f32)
     xt, pay_a, pay_b = call(
         edges_kernel,
         [block, pay_shape, pay_shape],
@@ -570,8 +583,10 @@
     later = call(
         later_kernel, [sds((T, C), f32)], [xt, *small], [*held, held_sems], hbm=range(1, 9), us=1
     )[0]
-    lon_shape = sds((3 * M + T, C), f32)
-    out_a, out_b = call(rows_kernel, [lon_shape] * 2, [xt, pay_a, later, got_a, got_b])
+    lon_shape = sds((2 * M + T, C), f32)
+    out_a, out_b, own = call(
+        rows_kernel, [lon_shape] * 2 + [sds((T, C), f32)], [xt, pay_a, later, got_a, got_b]
+    )
     got_y, got_x = swap(out_b, "lon", 1), swap(out_a, "lon", 0)
     state, edge = call(
         advect_kernel,
@@ -584,13 +599,14 @@
     table, count, *picked = call(
         tables_kernel,
         [sds((T, C), f32), sds((1,), jnp.int32), *chosen],
-        [pay_a, got_a, got_b, out_a, got_x, got_y, edge],
+        [pay_a, got_a, got_b, own, got_x, got_y, edge],
+        [VMEM((2, T, C), f32)],
         out_spaces=[VMEM, pltpu.SMEM, VMEM, VMEM, VMEM],
     )
     tab_b, tab_a = swap(table, "lat", 1), swap(table, "lat", 0)
     column = call(combine_kernel, [sds((T, C), f32)], [table, tab_a, tab_b], us=1)[0]
     col_y, col_x = swap(column, "lon", 1), swap(column, "lon", 0)
-    work = [VMEM((S, C), f32), VMEM((F, R, M, C), f32)]
+    work = [VMEM((S, C), f32), VMEM((S, C), f32), VMEM((F, R, M, C), f32)]
     state = call(
         first_kernel,
         [block],

time: 48.4 us -> 47.3 us (0.977)
  waiting for transfers between devices: 4.34 us -> 2.34 us
  starting transfers between devices: 20.5 us -> 21.4 us
    ppermute x8, waiting for transfers between devices: 4.34 us -> 2.34 us  [swap(): return lax.ppermute(x, axis, pairs)]
    ppermute x8, starting transfers between devices: 20.5 us -> 21.4 us  [swap(): return lax.ppermute(x, axis, pairs)]
  transfers between devices with their start and end apart: 8 -> 8, of which waited for: 3 -> 2; matrix products, arithmetic and copies ran while one was open for 0% -> 0% of each run, Pallas kernels for 23% -> 24%
where the time goes in v3:
time: 47.3 us; the launch traced here: 46.7 us
  Pallas kernels  22.6 us (48%)
  starting transfers between devices  21.4 us (45%)
  waiting for transfers between devices  2.34 us (5%)
    pallas_call x8, Pallas kernels, call(): pl.pallas_call(kernel, out_shape=outs, in_specs=[pl.BlockSpec(memory_spac...  22.6 us
    ppermute x8, starting transfers between devices, swap(): return lax.ppermute(x, axis, pairs)  21.4 us
    ppermute x8, waiting for transfers between devices, swap(): return lax.ppermute(x, axis, pairs)  2.34 us
  transfers between devices with their start and end apart: 8, of which 2 were waited for; matrix products, arithmetic and copies ran while one was open for 0% of the time, Pallas kernels for 24%

profile of v3, /device:TPU:111, one launch (start us, length us, event | category | flops | bytes accessed | tf_op | source)
XLA Modules:
  0.0 46.7 jit_solution(17175266386272225492)
XLA Ops:
  0.0 5.2 %edges_kernel.1 = (f32[3,32,80,128]{3,2,1,0:T(8,128)S(1)}, f32[432,128]{1,0:T(8,128)S(1)}, f32[432,128]{1,0:T(8,128)S(1)}) custom-call(f32[3,80,32,128]{3,2,1,0:T(8,128)} %refs_0_.1, s32[2,24]{1,0:T(2,128)} %refs_1_.3, s32[2,24]{1,0:T(2,128)} %refs_2_.3, f32[1,32,128]{2,1,0:T(8,128)} %cc_hbm.1, f32[1,32,128]{2,1,0:T(8,128)} %cr_hbm.1, f32[2,24]{1,0:T(2,128)} %refs_5_.3, ...), custom_call_target="tpu_custom_call" | custom-call | bytes 6000000 | tf_op jit(solution)/shard_map/edges_kernel/pallas_call | solution.py:540
  5.2 5.3 %collective-permute-start.1 = (f32[432,128]{1,0:T(8,128)S(1)}, f32[432,128]{1,0:T(8,128)S(1)}, u32[]{:S(2)}, u32[]{:S(2)}) collective-permute-start(f32[432,128]{1,0:T(8,128)S(1)} %get-tuple-element.19), channel_id=1, source_target_pairs={{16,32},{32,16},{48,64},{64,48},{80,96},{96,80},{112,128},{128,112... | collective-permute-start | bytes 663560 | tf_op jit(solution)/shard_map/ppermute | solution.py:556
  10.5 0.1 collective-permute-start
  10.6 2.9 %later_kernel.1.later = f32[112,128]{1,0:T(8,128)S(1)} custom-call(f32[3,32,80,128]{3,2,1,0:T(8,128)S(1)} %get-tuple-element.20.refs_0_.xt, s32[2,24]{1,0:T(2,128)} %refs_1_.3, s32[2,24]{1,0:T(2,128)} %refs_2_.3, f32[1,32,128]{2,1,0:T(8,128)} %cc_hbm.1, f32[1,32,128]{2,1,0:T(8,128)} %cr_hbm.1, f32[2,24]{1,0:T(2,128)} %refs_5_.3, f32[2,24]{1,0:T(2,128)} %refs_6_.3, ...), custom_call_target="tpu_custom_call" | custom-call | bytes 3000000 | tf_op jit(solution)/shard_map/later_kernel/pallas_call | solution.py:540
  13.5 0.6 %collective-permute-done.1.got_b = f32[432,128]{1,0:T(8,128)S(1)} collective-permute-done((f32[432,128]{1,0:T(8,128)S(1)}, f32[432,128]{1,0:T(8,128)S(1)}, u32[]{:S(2)}, u32[]{:S(2)}) %collective-permute-start.1) | collective-permute-done | bytes 221216 | tf_op jit(solution)/shard_map/ppermute | solution.py:556
  14.1 0.0 collective-permute-done.got_a
  14.1 0.5 %rows_kernel.1 = (f32[272,128]{1,0:T(8,128)S(1)}, f32[272,128]{1,0:T(8,128)S(1)}, f32[112,128]{1,0:T(8,128)S(1)}) custom-call(f32[3,32,80,128]{3,2,1,0:T(8,128)S(1)} %get-tuple-element.20.refs_0_.xt, f32[432,128]{1,0:T(8,128)S(1)} %get-tuple-element.18.pay, f32[112,128]{1,0:T(8,128)S(1)} %later_kernel.1.later, f32[432,128]{1,0:T(8,128)S(1)} %collective-permute-done.got_a, ...), custom_call_target="tpu_custom_call" | custom-call | bytes 6000000 | tf_op jit(solution)/shard_map/rows_kernel/pallas_call | solution.py:540
  14.6 0.3 collective-permute-start.2
  14.9 4.0 %collective-permute-start.3 = (f32[272,128]{1,0:T(8,128)S(1)}, f32[272,128]{1,0:T(8,128)S(1)}, u32[]{:S(2)}, u32[]{:S(2)}) collective-permute-start(f32[272,128]{1,0:T(8,128)S(1)} %get-tuple-element.23), channel_id=1, source_target_pairs={{1,2},{2,1},{3,4},{4,3},{5,6},{6,5},{7,8},{8,7},{9,10},{10,9},{11,... | collective-permute-start | bytes 417800 | tf_op jit(solution)/shard_map/ppermute | solution.py:556
  18.9 3.9 %advect_kernel.1 = (f32[3,32,80,128]{3,2,1,0:T(8,128)S(1)}, f32[32,128]{1,0:T(8,128)S(1)}) custom-call(f32[3,32,80,128]{3,2,1,0:T(8,128)S(1)} %get-tuple-element.20.refs_0_.xt, f32[432,128]{1,0:T(8,128)S(1)} %collective-permute-done.got_a, f32[432,128]{1,0:T(8,128)S(1)} %collective-permute-done.1.got_b, f32[1,32,128]{2,1,0:T(8,128)} %cc_hbm.1, ...), custom_call_target="tpu_custom_call" | custom-call | bytes 6000000 | tf_op jit(solution)/shard_map/advect_kernel/pallas_call | solution.py:540
  22.8 0.0 collective-permute-done.2.got_x
  22.9 0.0 collective-permute-done.3.got_y
  22.9 1.5 %tables_kernel.1 = (f32[112,128]{1,0:T(8,128)S(1)}, s32[1]{0:T(128)}, bf16[3,80,256]{2,1,0:T(8,128)(2,1)S(1)}, bf16[3,80,256]{2,1,0:T(8,128)(2,1)S(1)}, f32[3,3,80,128]{3,2,1,0:T(8,128)S(1)}) custom-call(f32[432,128]{1,0:T(8,128)S(1)} %get-tuple-element.18.pay, f32[432,128]{1,0:T(8,128)S(1)} %collective-permute-done.got_a, ...), custom_call_target="tpu_custom_call" | custom-call | bytes 6000000 | tf_op jit(solution)/shard_map/tables_kernel/pallas_call | solution.py:540
  24.3 5.4 %collective-permute-start.5 = (f32[112,128]{1,0:T(8,128)S(1)}, f32[112,128]{1,0:T(8,128)S(1)}, u32[]{:S(2)}, u32[]{:S(2)}) collective-permute-start(f32[112,128]{1,0:T(8,128)S(1)} %get-tuple-element.25.own), channel_id=1, source_target_pairs={{16,32},{32,16},{48,64},{64,48},{80,96},{96,80},{112,128},{128,112... | collective-permute-start | bytes 172040 | tf_op jit(solution)/shard_map/ppermute | solution.py:556
  29.8 0.1 collective-permute-start.4
  29.9 1.7 %collective-permute-done.5.b = f32[112,128]{1,0:T(8,128)S(1)} collective-permute-done((f32[112,128]{1,0:T(8,128)S(1)}, f32[112,128]{1,0:T(8,128)S(1)}, u32[]{:S(2)}, u32[]{:S(2)}) %collective-permute-start.5) | collective-permute-done | bytes 57376 | tf_op jit(solution)/shard_map/ppermute | solution.py:556
  31.6 0.0 collective-permute-done.4.a
  31.6 0.1 combine_kernel.1.own
  31.7 2.7 %collective-permute-start.7 = (f32[112,128]{1,0:T(8,128)S(1)}, f32[112,128]{1,0:T(8,128)S(1)}, u32[]{:S(2)}, u32[]{:S(2)}) collective-permute-start(f32[112,128]{1,0:T(8,128)S(1)} %combine_kernel.1.own), channel_id=1, source_target_pairs={{1,2},{2,1},{3,4},{4,3},{5,6},{6,5},{7,8},{8,7},{9,10},{10,9},{11,... | collective-permute-start | bytes 172040 | tf_op jit(solution)/shard_map/ppermute | solution.py:556
  34.4 3.5 %collective-permute-start.6 = (f32[112,128]{1,0:T(8,128)S(1)}, f32[112,128]{1,0:T(8,128)S(1)}, u32[]{:S(2)}, u32[]{:S(2)}) collective-permute-start(f32[112,128]{1,0:T(8,128)S(1)} %combine_kernel.1.own), channel_id=1, source_target_pairs={{0,1},{1,0},{2,3},{3,2},{4,5},{5,4},{6,7},{7,6},{8,9},{9,8},{10,11... | collective-permute-start | bytes 172040 | tf_op jit(solution)/shard_map/ppermute | solution.py:556
  37.9 4.2 %first_kernel.1.state = f32[3,32,80,128]{3,2,1,0:T(8,128)S(1)} custom-call(s32[1]{0:T(128)} %get-tuple-element.26.count, f32[3,32,80,128]{3,2,1,0:T(8,128)S(1)} %get-tuple-element.27.state, f32[32,128]{1,0:T(8,128)S(1)} %get-tuple-element.24.after.edge, f32[272,128]{1,0:T(8,128)S(1)} %collective-permute-done.2.got_x, ...), custom_call_target="tpu_custom_call" | custom-call | bytes 12000000 | tf_op jit(solution)/shard_map/first_kernel/pallas_call | solution.py:540
  42.2 0.0 collective-permute-done.7.got_y
  42.2 0.0 collective-permute-done.6.got_x
  42.2 4.3 %second_kernel.1 = f32[3,80,32,128]{3,2,1,0:T(8,128)} custom-call(f32[112,128]{1,0:T(8,128)S(1)} %combine_kernel.1.own, f32[112,128]{1,0:T(8,128)S(1)} %collective-permute-done.6.got_x, f32[112,128]{1,0:T(8,128)S(1)} %collective-permute-done.7.got_y, f32[3,32,80,128]{3,2,1,0:T(8,128)S(1)} %first_kernel.1.state), custom_call_target="tpu_custom_call" | custom-call | bytes 18000000 | tf_op jit(solution)/shard_map/second_kernel/pallas_call | solution.py:540
Async XLA Ops:
  5.2 8.9 %collective-permute-start.1 = (f32[432,128]{1,0:T(8,128)S(1)}, f32[432,128]{1,0:T(8,128)S(1)}, u32[]{:S(2)}, u32[]{:S(2)}) collective-permute-start(f32[432,128]{1,0:T(8,128)S(1)} %get-tuple-element.19), channel_id=1, source_target_pairs={{16,32},{32,16},{48,64},{64,48},{80,96},{96,80},{112,128},{128,112... | collective-permute-start | bytes 663560 | tf_op jit(solution)/shard_map/ppermute | solution.py:556
  10.5 3.6 %collective-permute-start = (f32[432,128]{1,0:T(8,128)S(1)}, f32[432,128]{1,0:T(8,128)S(1)}, u32[]{:S(2)}, u32[]{:S(2)}) collective-permute-start(f32[432,128]{1,0:T(8,128)S(1)} %get-tuple-element.18.pay), channel_id=1, source_target_pairs={{0,16},{16,0},{32,48},{48,32},{64,80},{80,64},{96,112},{112,96},{1... | collective-permute-start | bytes 663560 | tf_op jit(solution)/shard_map/ppermute | solution.py:556
  14.6 8.2 %collective-permute-start.2 = (f32[272,128]{1,0:T(8,128)S(1)}, f32[272,128]{1,0:T(8,128)S(1)}, u32[]{:S(2)}, u32[]{:S(2)}) collective-permute-start(f32[272,128]{1,0:T(8,128)S(1)} %get-tuple-element.22), channel_id=1, source_target_pairs={{0,1},{1,0},{2,3},{3,2},{4,5},{5,4},{6,7},{7,6},{8,9},{9,8},{10,11... | collective-permute-start | bytes 417800 | tf_op jit(solution)/shard_map/ppermute | solution.py:556
  14.9 8.0 %collective-permute-start.3 = (f32[272,128]{1,0:T(8,128)S(1)}, f32[272,128]{1,0:T(8,128)S(1)}, u32[]{:S(2)}, u32[]{:S(2)}) collective-permute-start(f32[272,128]{1,0:T(8,128)S(1)} %get-tuple-element.23), channel_id=1, source_target_pairs={{1,2},{2,1},{3,4},{4,3},{5,6},{6,5},{7,8},{8,7},{9,10},{10,9},{11,... | collective-permute-start | bytes 417800 | tf_op jit(solution)/shard_map/ppermute | solution.py:556
  24.3 7.3 %collective-permute-start.5 = (f32[112,128]{1,0:T(8,128)S(1)}, f32[112,128]{1,0:T(8,128)S(1)}, u32[]{:S(2)}, u32[]{:S(2)}) collective-permute-start(f32[112,128]{1,0:T(8,128)S(1)} %get-tuple-element.25.own), channel_id=1, source_target_pairs={{16,32},{32,16},{48,64},{64,48},{80,96},{96,80},{112,128},{128,112... | collective-permute-start | bytes 172040 | tf_op jit(solution)/shard_map/ppermute | solution.py:556
  29.8 1.9 %collective-permute-start.4 = (f32[112,128]{1,0:T(8,128)S(1)}, f32[112,128]{1,0:T(8,128)S(1)}, u32[]{:S(2)}, u32[]{:S(2)}) collective-permute-start(f32[112,128]{1,0:T(8,128)S(1)} %get-tuple-element.25.own), channel_id=1, source_target_pairs={{0,16},{16,0},{32,48},{48,32},{64,80},{80,64},{96,112},{112,96},{1... | collective-permute-start | bytes 172040 | tf_op jit(solution)/shard_map/ppermute | solution.py:556
  31.7 10.5 %collective-permute-start.7 = (f32[112,128]{1,0:T(8,128)S(1)}, f32[112,128]{1,0:T(8,128)S(1)}, u32[]{:S(2)}, u32[]{:S(2)}) collective-permute-start(f32[112,128]{1,0:T(8,128)S(1)} %combine_kernel.1.own), channel_id=1, source_target_pairs={{1,2},{2,1},{3,4},{4,3},{5,6},{6,5},{7,8},{8,7},{9,10},{10,9},{11,... | collective-permute-start | bytes 172040 | tf_op jit(solution)/shard_map/ppermute | solution.py:556
  34.4 7.8 %collective-permute-start.6 = (f32[112,128]{1,0:T(8,128)S(1)}, f32[112,128]{1,0:T(8,128)S(1)}, u32[]{:S(2)}, u32[]{:S(2)}) collective-permute-start(f32[112,128]{1,0:T(8,128)S(1)} %combine_kernel.1.own), channel_id=1, source_target_pairs={{0,1},{1,0},{2,3},{3,2},{4,5},{5,4},{6,7},{7,6},{8,9},{9,8},{10,11... | collective-permute-start | bytes 172040 | tf_op jit(solution)/shard_map/ppermute | solution.py:556
